TPU v7x, 32 devices: a whole 2x2x4 slice. The times are simulated.
32 devices in a mesh: row: 8 (over y, x, core), col: 4 (over z).
Axes of the slice: x: 2, y: 2, z: 4, core: 2. Of those that a mesh axis runs over, the one named last changes fastest.
Arguments:
- positions: float32 [3, 32768], P(None, ('row', 'col')), may hold values from -1 to 1
- normals: float32 [3, 32768], P(None, ('row', 'col')), may hold values from -4 to 4
- areas: float32 [32768], P(('row', 'col')), may hold values from 0.00012207031 to 0.0012207031
- direct: bfloat16 [32768, 64], P(('row', 'col')), may hold values from -6 to 6
- adjoint: bfloat16 [32768, 64], P(('row', 'col')), may hold values from -6 to 6
- spline: bfloat16 [32, 256, 512], P(('row', 'col')), may hold values from -0.375 to 0.375
- block_lists: int32 [128, 4], replicated, may hold values from 0 to 31, all different within a row
- patch_counts: int32 [64], replicated, may hold values from 1 to 8, 128 in all
- patch_owner: int32 [64], replicated, may hold values from 0 to 63, each once
Outputs:
- densities: float32 [32768], P(('row', 'col'))
- patch_grad: float32 [64, 512], P('row')
Inputs may be any that keep to these rules, and one draw needn't show every extreme that they name: `block_lists`: each row names 4 different spline blocks, and every spline block is named by some row. `patch_counts`: the counts sum to 128; the largest is exactly 8. `patch_owner`: A permutation of the patches.
All inputs are finite; a program needn't handle non-finite values.
Results may differ from a plain program's by a relative error of at most 0.0029.
Values may be sent and summed in bfloat16 or wider, within the bound.
A program may use at most 64 MiB of HBM per device.

v0:
```python
import jax
import jax.numpy as jnp
from jax import lax
from jax.sharding import PartitionSpec as P

BPAN = 256
NPATCH = 64
NBLK = 128


wave_number = 6.0
inv_four_pi = 0.07957747154594767


def kernel_block(tgt_pos, tgt_nrm, src_pos, src_area):
    depth_t = 0.5 * (tgt_pos[2] - 1.2)
    depth_s = 0.5 * (src_pos[2] - 1.2)
    delta_x = tgt_pos[0][:, None] - src_pos[0][None, :]
    delta_y = tgt_pos[1][:, None] - src_pos[1][None, :]
    delta_z = depth_t[:, None] - depth_s[None, :]
    image_z = depth_t[:, None] + depth_s[None, :]
    area_row = src_area[None, :]
    level = delta_x * delta_x + delta_y * delta_y
    near = level + delta_z * delta_z + area_row
    mirror = level + image_z * image_z + area_row
    slope = tgt_nrm[0][:, None] * delta_x + tgt_nrm[1][:, None] * delta_y
    vertical = tgt_nrm[2][:, None]
    rankine = (slope + vertical * delta_z) / (near * jnp.sqrt(near))
    reflect = (slope + vertical * image_z) / (mirror * jnp.sqrt(mirror))
    waves = (
        2.0
        * wave_number
        * jnp.exp(wave_number * image_z)
        * vertical
        * jnp.cos(wave_number * jnp.sqrt(level + area_row))
    )
    return area_row * (rankine + reflect - waves) * inv_four_pi


def on_device(
    positions, normals, areas, direct, adjoint, spline, block_lists, patch_counts, patch_owner
):
    tgt_pos, tgt_nrm = (
        lax.all_gather(positions, "col", axis=1, tiled=True),
        lax.all_gather(normals, "col", axis=1, tiled=True),
    )
    adj_tgt = lax.all_gather(adjoint, "col", axis=0, tiled=True)
    src_pos, src_area = (
        lax.all_gather(positions, "row", axis=1, tiled=True),
        lax.all_gather(areas, "row", axis=0, tiled=True),
    )
    dir_src = lax.all_gather(direct, "row", axis=0, tiled=True)
    targets = tgt_pos.shape[1]
    sources = src_pos.shape[1]
    columns = direct.shape[1]
    step_rows = min(targets, 256)
    count = targets // step_rows

    def advance(carry, index):
        start = index * step_rows
        part_pos = lax.dynamic_slice_in_dim(tgt_pos, start, step_rows, 1)
        part_nrm = lax.dynamic_slice_in_dim(tgt_nrm, start, step_rows, 1)
        adj_rows = lax.dynamic_slice_in_dim(adj_tgt, start, step_rows, 0)
        tile = kernel_block(part_pos, part_nrm, src_pos, src_area).astype(jnp.bfloat16)
        image_rows = jnp.dot(tile, dir_src, preferred_element_type=jnp.float32)
        carry = carry + lax.dot_general(
            tile, adj_rows, (((0,), (0,)), ((), ())), preferred_element_type=jnp.float32
        )
        return (carry, image_rows)

    adj_part, pieces = lax.scan(
        advance, jnp.zeros((sources, columns), jnp.float32), jnp.arange(count, dtype=jnp.int32)
    )
    dir_part = pieces.reshape(targets, columns)
    dir_mine = lax.psum_scatter(dir_part, "col", scatter_dimension=0, tiled=True)
    adj_mine = lax.psum_scatter(adj_part, "row", scatter_dimension=0, tiled=True)
    densities = jnp.sum(
        adjoint.astype(jnp.float32) * dir_mine + direct.astype(jnp.float32) * adj_mine, axis=1
    )
    every_density = lax.all_gather(densities, ("row", "col"), axis=0, tiled=True)
    blocks = every_density.reshape(NBLK, BPAN)
    ends = jnp.cumsum(patch_counts)
    starts = ends - patch_counts
    block_ids = jnp.arange(NBLK, dtype=jnp.int32)
    inside = (
        (starts[:, None] <= block_ids[None, :]) & (block_ids[None, :] < ends[:, None])
    ).astype(jnp.float32)
    owners = (patch_owner[None, :] == jnp.arange(NPATCH, dtype=jnp.int32)[:, None]).astype(
        jnp.float32
    )
    owned = jnp.dot(owners, inside, precision=lax.Precision.HIGHEST)
    holder = lax.axis_index(("row", "col"))
    listed = jnp.any(block_lists == holder, axis=1).astype(jnp.float32)
    weights = owned * listed[None, :]
    gathered = jnp.dot(weights, blocks, precision=lax.Precision.HIGHEST)
    contrib = jnp.dot(gathered, spline[0].astype(jnp.float32), precision=lax.Precision.HIGHEST)
    partial_rows = lax.psum_scatter(contrib, "row", scatter_dimension=0, tiled=True)
    patch_grad = lax.psum(partial_rows, "col")
    return (densities, patch_grad)


def solution(mesh):
    placed = (
        P(None, ("row", "col")),
        P(None, ("row", "col")),
        P(("row", "col")),
        P(("row", "col"), None),
        P(("row", "col"), None),
        P(("row", "col"), None, None),
        P(),
        P(),
        P(),
    )
    return jax.shard_map(
        on_device,
        mesh=mesh,
        in_specs=placed,
        out_specs=(P(("row", "col")), P("row", None)),
        check_vma=False,
    )
```

profile of v0, /device:TPU:0, one launch (start us, length us, event | category | flops | bytes accessed | tf_op | source)
XLA Modules:
  0.0 1781.1 jit_solution(15844026232613115796)
XLA Ops:
  7.2 1.8 copy.19
  9.1 1.1 copy.18
  10.2 10.7 all_gather.21
  20.9 13.6 all_gather.22
  34.5 13.3 all_gather.23
  47.8 9.0 all_gather.24
  56.8 22.6 %all_gather.25 = bf16[4096,64]{1,0:T(8,128)(2,1)S(1)} all-gather(bf16[1024,64]{1,0:T(8,128)(2,1)S(1)} %copy.18), channel_id=1, replica_groups=mesh['row'=8,'col'=4] {'col'}, dimensions={0}, use_global_device_ids=true | all-gather | bytes 655360 | tf_op jit(solution)/shard_map/all_gather | solution.py:47
  79.4 1502.3 %while.16 = (s32[]{:T(128)}, f32[8192,64]{0,1:T(8,128)}, f32[16,256,64]{1,0,2:T(8,128)S(1)}, f32[8192]{0:T(1024)S(1)}, s32[16]{0:T(128)S(1)}, /*index=5*/f32[3,4...) while((s32[]{:T(128)}, f32[8192,64]{0,1:T(8,128)}, ...), condition=%wide.region_1.2_spmd.clone, body=%wide.region_0.1_spmd.clone.sunk | while | flops 680542976 | bytes 18706728 | solution.py:71
  80.9 45.5 %convolution_add_fusion.2 = f32[8192,64]{0,1:T(8,128)} fusion(f32[8192,64]{0,1:T(8,128)} %get-tuple-element.317, pred[]{:T(512)S(6)} %compare.3, f32[256]{0:T(256)S(1)} %broadcast_multiply_fusion.2, f32[8192]{0:T(1024)S(1)} %bitcast.57, f32[256]{0:T(256)S(1)} %bitcast.68, f32[256]{0:T(256)S(1)} %bitcast.62, f32[8192]{0:T(1024)S(1)} %bitcast.59, ...), kind=kOutput, calls=%fused_computation.11.clone.3 | convolution fusion | flops 340787200 | bytes 4398085 | tf_op jit(solution)/shard_map/while/body/eval_jaxpr/dot_general | solution.py:66
  126.4 43.4 %fusion.66 = bf16[256,8192]{1,0:T(8,128)(2,1)S(1)} fusion(f32[256]{0:T(256)S(1)} %broadcast_multiply_fusion.2, f32[8192]{0:T(1024)S(1)} %bitcast.58, f32[256]{0:T(256)S(1)} %bitcast.69, f32[256]{0:T(256)S(1)} %bitcast.63, f32[8192]{0:T(1024)S(1)} %bitcast.60, f32[256]{0:T(256)S(1)} %bitcast.67, f32[256]{0:T(256)S(1)} %bitcast.71, ...), kind=kLoop, calls=%fused_computation.33.clone.clone.1.clone.1 | loop fusion | flops 71303168 | bytes 4332544 | tf_op jit(solution)/shard_map/while/body/eval_jaxpr/dot_general | solution.py:65
  169.8 1.4 convolution_bitcast_fusion.2
  173.7 46.7 %convolution_add_fusion.2 = f32[8192,64]{0,1:T(8,128)} fusion(f32[8192,64]{0,1:T(8,128)} %get-tuple-element.317, pred[]{:T(512)S(6)} %compare.3, f32[256]{0:T(256)S(1)} %broadcast_multiply_fusion.2, f32[8192]{0:T(1024)S(1)} %bitcast.57, f32[256]{0:T(256)S(1)} %bitcast.68, f32[256]{0:T(256)S(1)} %bitcast.62, f32[8192]{0:T(1024)S(1)} %bitcast.59, ...), kind=kOutput, calls=%fused_computation.11.clone.3 | convolution fusion | flops 340787200 | bytes 4398085 | tf_op jit(solution)/shard_map/while/body/eval_jaxpr/dot_general | solution.py:66
  220.4 43.4 %fusion.66 = bf16[256,8192]{1,0:T(8,128)(2,1)S(1)} fusion(f32[256]{0:T(256)S(1)} %broadcast_multiply_fusion.2, f32[8192]{0:T(1024)S(1)} %bitcast.58, f32[256]{0:T(256)S(1)} %bitcast.69, f32[256]{0:T(256)S(1)} %bitcast.63, f32[8192]{0:T(1024)S(1)} %bitcast.60, f32[256]{0:T(256)S(1)} %bitcast.67, f32[256]{0:T(256)S(1)} %bitcast.71, ...), kind=kLoop, calls=%fused_computation.33.clone.clone.1.clone.1 | loop fusion | flops 71303168 | bytes 4332544 | tf_op jit(solution)/shard_map/while/body/eval_jaxpr/dot_general | solution.py:65
  263.8 1.4 convolution_bitcast_fusion.2
  267.6 46.7 %convolution_add_fusion.2 = f32[8192,64]{0,1:T(8,128)} fusion(f32[8192,64]{0,1:T(8,128)} %get-tuple-element.317, pred[]{:T(512)S(6)} %compare.3, f32[256]{0:T(256)S(1)} %broadcast_multiply_fusion.2, f32[8192]{0:T(1024)S(1)} %bitcast.57, f32[256]{0:T(256)S(1)} %bitcast.68, f32[256]{0:T(256)S(1)} %bitcast.62, f32[8192]{0:T(1024)S(1)} %bitcast.59, ...), kind=kOutput, calls=%fused_computation.11.clone.3 | convolution fusion | flops 340787200 | bytes 4398085 | tf_op jit(solution)/shard_map/while/body/eval_jaxpr/dot_general | solution.py:66
  314.4 43.4 %fusion.66 = bf16[256,8192]{1,0:T(8,128)(2,1)S(1)} fusion(f32[256]{0:T(256)S(1)} %broadcast_multiply_fusion.2, f32[8192]{0:T(1024)S(1)} %bitcast.58, f32[256]{0:T(256)S(1)} %bitcast.69, f32[256]{0:T(256)S(1)} %bitcast.63, f32[8192]{0:T(1024)S(1)} %bitcast.60, f32[256]{0:T(256)S(1)} %bitcast.67, f32[256]{0:T(256)S(1)} %bitcast.71, ...), kind=kLoop, calls=%fused_computation.33.clone.clone.1.clone.1 | loop fusion | flops 71303168 | bytes 4332544 | tf_op jit(solution)/shard_map/while/body/eval_jaxpr/dot_general | solution.py:65
  357.8 1.4 convolution_bitcast_fusion.2
  361.6 46.7 %convolution_add_fusion.2 = f32[8192,64]{0,1:T(8,128)} fusion(f32[8192,64]{0,1:T(8,128)} %get-tuple-element.317, pred[]{:T(512)S(6)} %compare.3, f32[256]{0:T(256)S(1)} %broadcast_multiply_fusion.2, f32[8192]{0:T(1024)S(1)} %bitcast.57, f32[256]{0:T(256)S(1)} %bitcast.68, f32[256]{0:T(256)S(1)} %bitcast.62, f32[8192]{0:T(1024)S(1)} %bitcast.59, ...), kind=kOutput, calls=%fused_computation.11.clone.3 | convolution fusion | flops 340787200 | bytes 4398085 | tf_op jit(solution)/shard_map/while/body/eval_jaxpr/dot_general | solution.py:66
  408.3 43.4 %fusion.66 = bf16[256,8192]{1,0:T(8,128)(2,1)S(1)} fusion(f32[256]{0:T(256)S(1)} %broadcast_multiply_fusion.2, f32[8192]{0:T(1024)S(1)} %bitcast.58, f32[256]{0:T(256)S(1)} %bitcast.69, f32[256]{0:T(256)S(1)} %bitcast.63, f32[8192]{0:T(1024)S(1)} %bitcast.60, f32[256]{0:T(256)S(1)} %bitcast.67, f32[256]{0:T(256)S(1)} %bitcast.71, ...), kind=kLoop, calls=%fused_computation.33.clone.clone.1.clone.1 | loop fusion | flops 71303168 | bytes 4332544 | tf_op jit(solution)/shard_map/while/body/eval_jaxpr/dot_general | solution.py:65
  451.7 1.4 convolution_bitcast_fusion.2
  455.6 46.7 %convolution_add_fusion.2 = f32[8192,64]{0,1:T(8,128)} fusion(f32[8192,64]{0,1:T(8,128)} %get-tuple-element.317, pred[]{:T(512)S(6)} %compare.3, f32[256]{0:T(256)S(1)} %broadcast_multiply_fusion.2, f32[8192]{0:T(1024)S(1)} %bitcast.57, f32[256]{0:T(256)S(1)} %bitcast.68, f32[256]{0:T(256)S(1)} %bitcast.62, f32[8192]{0:T(1024)S(1)} %bitcast.59, ...), kind=kOutput, calls=%fused_computation.11.clone.3 | convolution fusion | flops 340787200 | bytes 4398085 | tf_op jit(solution)/shard_map/while/body/eval_jaxpr/dot_general | solution.py:66
  502.3 43.4 %fusion.66 = bf16[256,8192]{1,0:T(8,128)(2,1)S(1)} fusion(f32[256]{0:T(256)S(1)} %broadcast_multiply_fusion.2, f32[8192]{0:T(1024)S(1)} %bitcast.58, f32[256]{0:T(256)S(1)} %bitcast.69, f32[256]{0:T(256)S(1)} %bitcast.63, f32[8192]{0:T(1024)S(1)} %bitcast.60, f32[256]{0:T(256)S(1)} %bitcast.67, f32[256]{0:T(256)S(1)} %bitcast.71, ...), kind=kLoop, calls=%fused_computation.33.clone.clone.1.clone.1 | loop fusion | flops 71303168 | bytes 4332544 | tf_op jit(solution)/shard_map/while/body/eval_jaxpr/dot_general | solution.py:65
  545.7 1.4 convolution_bitcast_fusion.2
  549.5 46.7 %convolution_add_fusion.2 = f32[8192,64]{0,1:T(8,128)} fusion(f32[8192,64]{0,1:T(8,128)} %get-tuple-element.317, pred[]{:T(512)S(6)} %compare.3, f32[256]{0:T(256)S(1)} %broadcast_multiply_fusion.2, f32[8192]{0:T(1024)S(1)} %bitcast.57, f32[256]{0:T(256)S(1)} %bitcast.68, f32[256]{0:T(256)S(1)} %bitcast.62, f32[8192]{0:T(1024)S(1)} %bitcast.59, ...), kind=kOutput, calls=%fused_computation.11.clone.3 | convolution fusion | flops 340787200 | bytes 4398085 | tf_op jit(solution)/shard_map/while/body/eval_jaxpr/dot_general | solution.py:66
  596.3 43.4 %fusion.66 = bf16[256,8192]{1,0:T(8,128)(2,1)S(1)} fusion(f32[256]{0:T(256)S(1)} %broadcast_multiply_fusion.2, f32[8192]{0:T(1024)S(1)} %bitcast.58, f32[256]{0:T(256)S(1)} %bitcast.69, f32[256]{0:T(256)S(1)} %bitcast.63, f32[8192]{0:T(1024)S(1)} %bitcast.60, f32[256]{0:T(256)S(1)} %bitcast.67, f32[256]{0:T(256)S(1)} %bitcast.71, ...), kind=kLoop, calls=%fused_computation.33.clone.clone.1.clone.1 | loop fusion | flops 71303168 | bytes 4332544 | tf_op jit(solution)/shard_map/while/body/eval_jaxpr/dot_general | solution.py:65
  639.7 1.4 convolution_bitcast_fusion.2
  643.5 46.7 %convolution_add_fusion.2 = f32[8192,64]{0,1:T(8,128)} fusion(f32[8192,64]{0,1:T(8,128)} %get-tuple-element.317, pred[]{:T(512)S(6)} %compare.3, f32[256]{0:T(256)S(1)} %broadcast_multiply_fusion.2, f32[8192]{0:T(1024)S(1)} %bitcast.57, f32[256]{0:T(256)S(1)} %bitcast.68, f32[256]{0:T(256)S(1)} %bitcast.62, f32[8192]{0:T(1024)S(1)} %bitcast.59, ...), kind=kOutput, calls=%fused_computation.11.clone.3 | convolution fusion | flops 340787200 | bytes 4398085 | tf_op jit(solution)/shard_map/while/body/eval_jaxpr/dot_general | solution.py:66
  690.2 43.4 %fusion.66 = bf16[256,8192]{1,0:T(8,128)(2,1)S(1)} fusion(f32[256]{0:T(256)S(1)} %broadcast_multiply_fusion.2, f32[8192]{0:T(1024)S(1)} %bitcast.58, f32[256]{0:T(256)S(1)} %bitcast.69, f32[256]{0:T(256)S(1)} %bitcast.63, f32[8192]{0:T(1024)S(1)} %bitcast.60, f32[256]{0:T(256)S(1)} %bitcast.67, f32[256]{0:T(256)S(1)} %bitcast.71, ...), kind=kLoop, calls=%fused_computation.33.clone.clone.1.clone.1 | loop fusion | flops 71303168 | bytes 4332544 | tf_op jit(solution)/shard_map/while/body/eval_jaxpr/dot_general | solution.py:65
  733.7 1.4 convolution_bitcast_fusion.2
  737.5 46.7 %convolution_add_fusion.2 = f32[8192,64]{0,1:T(8,128)} fusion(f32[8192,64]{0,1:T(8,128)} %get-tuple-element.317, pred[]{:T(512)S(6)} %compare.3, f32[256]{0:T(256)S(1)} %broadcast_multiply_fusion.2, f32[8192]{0:T(1024)S(1)} %bitcast.57, f32[256]{0:T(256)S(1)} %bitcast.68, f32[256]{0:T(256)S(1)} %bitcast.62, f32[8192]{0:T(1024)S(1)} %bitcast.59, ...), kind=kOutput, calls=%fused_computation.11.clone.3 | convolution fusion | flops 340787200 | bytes 4398085 | tf_op jit(solution)/shard_map/while/body/eval_jaxpr/dot_general | solution.py:66
  784.2 43.4 %fusion.66 = bf16[256,8192]{1,0:T(8,128)(2,1)S(1)} fusion(f32[256]{0:T(256)S(1)} %broadcast_multiply_fusion.2, f32[8192]{0:T(1024)S(1)} %bitcast.58, f32[256]{0:T(256)S(1)} %bitcast.69, f32[256]{0:T(256)S(1)} %bitcast.63, f32[8192]{0:T(1024)S(1)} %bitcast.60, f32[256]{0:T(256)S(1)} %bitcast.67, f32[256]{0:T(256)S(1)} %bitcast.71, ...), kind=kLoop, calls=%fused_computation.33.clone.clone.1.clone.1 | loop fusion | flops 71303168 | bytes 4332544 | tf_op jit(solution)/shard_map/while/body/eval_jaxpr/dot_general | solution.py:65
  827.6 1.4 convolution_bitcast_fusion.2
  831.5 46.7 %convolution_add_fusion.2 = f32[8192,64]{0,1:T(8,128)} fusion(f32[8192,64]{0,1:T(8,128)} %get-tuple-element.317, pred[]{:T(512)S(6)} %compare.3, f32[256]{0:T(256)S(1)} %broadcast_multiply_fusion.2, f32[8192]{0:T(1024)S(1)} %bitcast.57, f32[256]{0:T(256)S(1)} %bitcast.68, f32[256]{0:T(256)S(1)} %bitcast.62, f32[8192]{0:T(1024)S(1)} %bitcast.59, ...), kind=kOutput, calls=%fused_computation.11.clone.3 | convolution fusion | flops 340787200 | bytes 4398085 | tf_op jit(solution)/shard_map/while/body/eval_jaxpr/dot_general | solution.py:66
  878.2 43.4 %fusion.66 = bf16[256,8192]{1,0:T(8,128)(2,1)S(1)} fusion(f32[256]{0:T(256)S(1)} %broadcast_multiply_fusion.2, f32[8192]{0:T(1024)S(1)} %bitcast.58, f32[256]{0:T(256)S(1)} %bitcast.69, f32[256]{0:T(256)S(1)} %bitcast.63, f32[8192]{0:T(1024)S(1)} %bitcast.60, f32[256]{0:T(256)S(1)} %bitcast.67, f32[256]{0:T(256)S(1)} %bitcast.71, ...), kind=kLoop, calls=%fused_computation.33.clone.clone.1.clone.1 | loop fusion | flops 71303168 | bytes 4332544 | tf_op jit(solution)/shard_map/while/body/eval_jaxpr/dot_general | solution.py:65
  921.6 1.4 convolution_bitcast_fusion.2
  925.4 46.7 %convolution_add_fusion.2 = f32[8192,64]{0,1:T(8,128)} fusion(f32[8192,64]{0,1:T(8,128)} %get-tuple-element.317, pred[]{:T(512)S(6)} %compare.3, f32[256]{0:T(256)S(1)} %broadcast_multiply_fusion.2, f32[8192]{0:T(1024)S(1)} %bitcast.57, f32[256]{0:T(256)S(1)} %bitcast.68, f32[256]{0:T(256)S(1)} %bitcast.62, f32[8192]{0:T(1024)S(1)} %bitcast.59, ...), kind=kOutput, calls=%fused_computation.11.clone.3 | convolution fusion | flops 340787200 | bytes 4398085 | tf_op jit(solution)/shard_map/while/body/eval_jaxpr/dot_general | solution.py:66
  972.2 43.4 %fusion.66 = bf16[256,8192]{1,0:T(8,128)(2,1)S(1)} fusion(f32[256]{0:T(256)S(1)} %broadcast_multiply_fusion.2, f32[8192]{0:T(1024)S(1)} %bitcast.58, f32[256]{0:T(256)S(1)} %bitcast.69, f32[256]{0:T(256)S(1)} %bitcast.63, f32[8192]{0:T(1024)S(1)} %bitcast.60, f32[256]{0:T(256)S(1)} %bitcast.67, f32[256]{0:T(256)S(1)} %bitcast.71, ...), kind=kLoop, calls=%fused_computation.33.clone.clone.1.clone.1 | loop fusion | flops 71303168 | bytes 4332544 | tf_op jit(solution)/shard_map/while/body/eval_jaxpr/dot_general | solution.py:65
  1015.6 1.4 convolution_bitcast_fusion.2
  1019.4 46.7 %convolution_add_fusion.2 = f32[8192,64]{0,1:T(8,128)} fusion(f32[8192,64]{0,1:T(8,128)} %get-tuple-element.317, pred[]{:T(512)S(6)} %compare.3, f32[256]{0:T(256)S(1)} %broadcast_multiply_fusion.2, f32[8192]{0:T(1024)S(1)} %bitcast.57, f32[256]{0:T(256)S(1)} %bitcast.68, f32[256]{0:T(256)S(1)} %bitcast.62, f32[8192]{0:T(1024)S(1)} %bitcast.59, ...), kind=kOutput, calls=%fused_computation.11.clone.3 | convolution fusion | flops 340787200 | bytes 4398085 | tf_op jit(solution)/shard_map/while/body/eval_jaxpr/dot_general | solution.py:66
  1066.1 43.4 %fusion.66 = bf16[256,8192]{1,0:T(8,128)(2,1)S(1)} fusion(f32[256]{0:T(256)S(1)} %broadcast_multiply_fusion.2, f32[8192]{0:T(1024)S(1)} %bitcast.58, f32[256]{0:T(256)S(1)} %bitcast.69, f32[256]{0:T(256)S(1)} %bitcast.63, f32[8192]{0:T(1024)S(1)} %bitcast.60, f32[256]{0:T(256)S(1)} %bitcast.67, f32[256]{0:T(256)S(1)} %bitcast.71, ...), kind=kLoop, calls=%fused_computation.33.clone.clone.1.clone.1 | loop fusion | flops 71303168 | bytes 4332544 | tf_op jit(solution)/shard_map/while/body/eval_jaxpr/dot_general | solution.py:65
  1109.5 1.4 convolution_bitcast_fusion.2
  1113.4 46.7 %convolution_add_fusion.2 = f32[8192,64]{0,1:T(8,128)} fusion(f32[8192,64]{0,1:T(8,128)} %get-tuple-element.317, pred[]{:T(512)S(6)} %compare.3, f32[256]{0:T(256)S(1)} %broadcast_multiply_fusion.2, f32[8192]{0:T(1024)S(1)} %bitcast.57, f32[256]{0:T(256)S(1)} %bitcast.68, f32[256]{0:T(256)S(1)} %bitcast.62, f32[8192]{0:T(1024)S(1)} %bitcast.59, ...), kind=kOutput, calls=%fused_computation.11.clone.3 | convolution fusion | flops 340787200 | bytes 4398085 | tf_op jit(solution)/shard_map/while/body/eval_jaxpr/dot_general | solution.py:66
  1160.1 43.4 %fusion.66 = bf16[256,8192]{1,0:T(8,128)(2,1)S(1)} fusion(f32[256]{0:T(256)S(1)} %broadcast_multiply_fusion.2, f32[8192]{0:T(1024)S(1)} %bitcast.58, f32[256]{0:T(256)S(1)} %bitcast.69, f32[256]{0:T(256)S(1)} %bitcast.63, f32[8192]{0:T(1024)S(1)} %bitcast.60, f32[256]{0:T(256)S(1)} %bitcast.67, f32[256]{0:T(256)S(1)} %bitcast.71, ...), kind=kLoop, calls=%fused_computation.33.clone.clone.1.clone.1 | loop fusion | flops 71303168 | bytes 4332544 | tf_op jit(solution)/shard_map/while/body/eval_jaxpr/dot_general | solution.py:65
  1203.5 1.4 convolution_bitcast_fusion.2
  1207.3 46.7 %convolution_add_fusion.2 = f32[8192,64]{0,1:T(8,128)} fusion(f32[8192,64]{0,1:T(8,128)} %get-tuple-element.317, pred[]{:T(512)S(6)} %compare.3, f32[256]{0:T(256)S(1)} %broadcast_multiply_fusion.2, f32[8192]{0:T(1024)S(1)} %bitcast.57, f32[256]{0:T(256)S(1)} %bitcast.68, f32[256]{0:T(256)S(1)} %bitcast.62, f32[8192]{0:T(1024)S(1)} %bitcast.59, ...), kind=kOutput, calls=%fused_computation.11.clone.3 | convolution fusion | flops 340787200 | bytes 4398085 | tf_op jit(solution)/shard_map/while/body/eval_jaxpr/dot_general | solution.py:66
  1254.1 43.4 %fusion.66 = bf16[256,8192]{1,0:T(8,128)(2,1)S(1)} fusion(f32[256]{0:T(256)S(1)} %broadcast_multiply_fusion.2, f32[8192]{0:T(1024)S(1)} %bitcast.58, f32[256]{0:T(256)S(1)} %bitcast.69, f32[256]{0:T(256)S(1)} %bitcast.63, f32[8192]{0:T(1024)S(1)} %bitcast.60, f32[256]{0:T(256)S(1)} %bitcast.67, f32[256]{0:T(256)S(1)} %bitcast.71, ...), kind=kLoop, calls=%fused_computation.33.clone.clone.1.clone.1 | loop fusion | flops 71303168 | bytes 4332544 | tf_op jit(solution)/shard_map/while/body/eval_jaxpr/dot_general | solution.py:65
  1297.5 1.4 convolution_bitcast_fusion.2
  1301.3 46.7 %convolution_add_fusion.2 = f32[8192,64]{0,1:T(8,128)} fusion(f32[8192,64]{0,1:T(8,128)} %get-tuple-element.317, pred[]{:T(512)S(6)} %compare.3, f32[256]{0:T(256)S(1)} %broadcast_multiply_fusion.2, f32[8192]{0:T(1024)S(1)} %bitcast.57, f32[256]{0:T(256)S(1)} %bitcast.68, f32[256]{0:T(256)S(1)} %bitcast.62, f32[8192]{0:T(1024)S(1)} %bitcast.59, ...), kind=kOutput, calls=%fused_computation.11.clone.3 | convolution fusion | flops 340787200 | bytes 4398085 | tf_op jit(solution)/shard_map/while/body/eval_jaxpr/dot_general | solution.py:66
  1348.0 43.4 %fusion.66 = bf16[256,8192]{1,0:T(8,128)(2,1)S(1)} fusion(f32[256]{0:T(256)S(1)} %broadcast_multiply_fusion.2, f32[8192]{0:T(1024)S(1)} %bitcast.58, f32[256]{0:T(256)S(1)} %bitcast.69, f32[256]{0:T(256)S(1)} %bitcast.63, f32[8192]{0:T(1024)S(1)} %bitcast.60, f32[256]{0:T(256)S(1)} %bitcast.67, f32[256]{0:T(256)S(1)} %bitcast.71, ...), kind=kLoop, calls=%fused_computation.33.clone.clone.1.clone.1 | loop fusion | flops 71303168 | bytes 4332544 | tf_op jit(solution)/shard_map/while/body/eval_jaxpr/dot_general | solution.py:65
  1391.5 1.4 convolution_bitcast_fusion.2
  1395.3 46.7 %convolution_add_fusion.2 = f32[8192,64]{0,1:T(8,128)} fusion(f32[8192,64]{0,1:T(8,128)} %get-tuple-element.317, pred[]{:T(512)S(6)} %compare.3, f32[256]{0:T(256)S(1)} %broadcast_multiply_fusion.2, f32[8192]{0:T(1024)S(1)} %bitcast.57, f32[256]{0:T(256)S(1)} %bitcast.68, f32[256]{0:T(256)S(1)} %bitcast.62, f32[8192]{0:T(1024)S(1)} %bitcast.59, ...), kind=kOutput, calls=%fused_computation.11.clone.3 | convolution fusion | flops 340787200 | bytes 4398085 | tf_op jit(solution)/shard_map/while/body/eval_jaxpr/dot_general | solution.py:66
  1442.0 43.4 %fusion.66 = bf16[256,8192]{1,0:T(8,128)(2,1)S(1)} fusion(f32[256]{0:T(256)S(1)} %broadcast_multiply_fusion.2, f32[8192]{0:T(1024)S(1)} %bitcast.58, f32[256]{0:T(256)S(1)} %bitcast.69, f32[256]{0:T(256)S(1)} %bitcast.63, f32[8192]{0:T(1024)S(1)} %bitcast.60, f32[256]{0:T(256)S(1)} %bitcast.67, f32[256]{0:T(256)S(1)} %bitcast.71, ...), kind=kLoop, calls=%fused_computation.33.clone.clone.1.clone.1 | loop fusion | flops 71303168 | bytes 4332544 | tf_op jit(solution)/shard_map/while/body/eval_jaxpr/dot_general | solution.py:65
  1485.4 1.4 convolution_bitcast_fusion.2
  1489.3 46.7 %convolution_add_fusion.2 = f32[8192,64]{0,1:T(8,128)} fusion(f32[8192,64]{0,1:T(8,128)} %get-tuple-element.317, pred[]{:T(512)S(6)} %compare.3, f32[256]{0:T(256)S(1)} %broadcast_multiply_fusion.2, f32[8192]{0:T(1024)S(1)} %bitcast.57, f32[256]{0:T(256)S(1)} %bitcast.68, f32[256]{0:T(256)S(1)} %bitcast.62, f32[8192]{0:T(1024)S(1)} %bitcast.59, ...), kind=kOutput, calls=%fused_computation.11.clone.3 | convolution fusion | flops 340787200 | bytes 4398085 | tf_op jit(solution)/shard_map/while/body/eval_jaxpr/dot_general | solution.py:66
  1536.0 43.4 %fusion.66 = bf16[256,8192]{1,0:T(8,128)(2,1)S(1)} fusion(f32[256]{0:T(256)S(1)} %broadcast_multiply_fusion.2, f32[8192]{0:T(1024)S(1)} %bitcast.58, f32[256]{0:T(256)S(1)} %bitcast.69, f32[256]{0:T(256)S(1)} %bitcast.63, f32[8192]{0:T(1024)S(1)} %bitcast.60, f32[256]{0:T(256)S(1)} %bitcast.67, f32[256]{0:T(256)S(1)} %bitcast.71, ...), kind=kLoop, calls=%fused_computation.33.clone.clone.1.clone.1 | loop fusion | flops 71303168 | bytes 4332544 | tf_op jit(solution)/shard_map/while/body/eval_jaxpr/dot_general | solution.py:65
  1579.4 1.4 convolution_bitcast_fusion.2
  1581.8 1.6 copy.25
  1584.8 25.8 %reduce-scatter.4.cloned.1.call-done = f32[1024,64]{0,1:T(8,128)} async-done(((f32[4096,64]{0,1:T(8,128)}), f32[1024,64]{0,1:T(8,128)}) %reduce-scatter.4.cloned.1.call-update) | async-done | bytes 262160 | tf_op jit(solution)/shard_map/reduce_scatter | solution.py:75
  1610.6 42.9 %reduce-scatter.6.cloned.1.call-done = f32[1024,64]{0,1:T(8,128)} async-done(((f32[8192,64]{0,1:T(8,128)}), f32[1024,64]{0,1:T(8,128)}) %reduce-scatter.6.cloned.1.call-update) | async-done | bytes 262160 | tf_op jit(solution)/shard_map/reduce_scatter | solution.py:76
  1653.5 1.1 add_reduce_fusion
  1654.6 67.8 %all_gather.27 = f32[32768]{0:T(1024)S(1)} all-gather(f32[1024]{0:T(1024)S(1)} %add_reduce_fusion), channel_id=1, replica_groups=mesh['row'=8,'col'=4] {'row','col'}, dimensions={0}, use_global_device_ids=true | all-gather | bytes 135168 | tf_op jit(solution)/shard_map/all_gather | solution.py:80
  1722.7 0.9 fusion.31
  1723.6 31.0 %reduce-scatter.8.cloned.1.call-done = f32[8,512]{1,0:T(8,128)} async-done(((f32[64,512]{1,0:T(8,128)}), f32[8,512]{1,0:T(8,128)}) %reduce-scatter.8.cloned.1.call-update) | async-done | bytes 16400 | tf_op jit(solution)/shard_map/reduce_scatter | solution.py:97
  1754.6 19.9 %psum.7 = f32[8,512]{1,0:T(8,128)} all-reduce(f32[8,512]{1,0:T(8,128)} %reduce-scatter.8.cloned.1.call-done), channel_id=1, replica_groups=mesh['row'=8,'col'=4] {'col'}, use_global_device_ids=true, to_apply=%region_8.9 | all-reduce | flops 4096 | bytes 32768 | tf_op jit(solution)/shard_map/psum | solution.py:98
  (163 shorter events, 29.4 us)
Async XLA Ops:
  7.2 1715.5 %copy-start = (bf16[1,256,512]{2,1,0:T(8,128)(2,1)S(1)}, bf16[1,256,512]{2,1,0:T(8,128)(2,1)}, u32[]{:S(2)}) copy-start(bf16[1,256,512]{2,1,0:T(8,128)(2,1)} %param.16) | copy-start | bytes 786436
  7.2 72.3 %all-gather.2.cloned.1.call-start = ((), (), s32[]{:S(2)}) async-start(), calls=%async_computation.3 | async-start | bytes 2359296 | tf_op jit(solution)/shard_map/all_gather | solution.py:52
  9.0 1601.6 %reduce-scatter.4.cloned.1.call-start = ((), (), s32[]{:S(2)}) async-start(), calls=%async_computation.4 | async-start | bytes 1310720 | tf_op jit(solution)/shard_map/reduce_scatter | solution.py:75
  126.4 43.4 %copy-start.1 = (bf16[8192,64]{1,0:T(8,128)(2,1)S(1)}, bf16[8192,64]{1,0:T(8,128)(2,1)}, u32[]{:S(2)}) copy-start(bf16[8192,64]{1,0:T(8,128)(2,1)} %get-tuple-element.341) | copy-start | bytes 3145732 | tf_op jit(solution)/shard_map/while
  220.4 43.4 %copy-start.1 = (bf16[8192,64]{1,0:T(8,128)(2,1)S(1)}, bf16[8192,64]{1,0:T(8,128)(2,1)}, u32[]{:S(2)}) copy-start(bf16[8192,64]{1,0:T(8,128)(2,1)} %get-tuple-element.341) | copy-start | bytes 3145732 | tf_op jit(solution)/shard_map/while
  314.4 43.4 %copy-start.1 = (bf16[8192,64]{1,0:T(8,128)(2,1)S(1)}, bf16[8192,64]{1,0:T(8,128)(2,1)}, u32[]{:S(2)}) copy-start(bf16[8192,64]{1,0:T(8,128)(2,1)} %get-tuple-element.341) | copy-start | bytes 3145732 | tf_op jit(solution)/shard_map/while
  408.3 43.4 %copy-start.1 = (bf16[8192,64]{1,0:T(8,128)(2,1)S(1)}, bf16[8192,64]{1,0:T(8,128)(2,1)}, u32[]{:S(2)}) copy-start(bf16[8192,64]{1,0:T(8,128)(2,1)} %get-tuple-element.341) | copy-start | bytes 3145732 | tf_op jit(solution)/shard_map/while
  502.3 43.4 %copy-start.1 = (bf16[8192,64]{1,0:T(8,128)(2,1)S(1)}, bf16[8192,64]{1,0:T(8,128)(2,1)}, u32[]{:S(2)}) copy-start(bf16[8192,64]{1,0:T(8,128)(2,1)} %get-tuple-element.341) | copy-start | bytes 3145732 | tf_op jit(solution)/shard_map/while
  596.3 43.4 %copy-start.1 = (bf16[8192,64]{1,0:T(8,128)(2,1)S(1)}, bf16[8192,64]{1,0:T(8,128)(2,1)}, u32[]{:S(2)}) copy-start(bf16[8192,64]{1,0:T(8,128)(2,1)} %get-tuple-element.341) | copy-start | bytes 3145732 | tf_op jit(solution)/shard_map/while
  690.2 43.4 %copy-start.1 = (bf16[8192,64]{1,0:T(8,128)(2,1)S(1)}, bf16[8192,64]{1,0:T(8,128)(2,1)}, u32[]{:S(2)}) copy-start(bf16[8192,64]{1,0:T(8,128)(2,1)} %get-tuple-element.341) | copy-start | bytes 3145732 | tf_op jit(solution)/shard_map/while
  784.2 43.4 %copy-start.1 = (bf16[8192,64]{1,0:T(8,128)(2,1)S(1)}, bf16[8192,64]{1,0:T(8,128)(2,1)}, u32[]{:S(2)}) copy-start(bf16[8192,64]{1,0:T(8,128)(2,1)} %get-tuple-element.341) | copy-start | bytes 3145732 | tf_op jit(solution)/shard_map/while
  878.2 43.4 %copy-start.1 = (bf16[8192,64]{1,0:T(8,128)(2,1)S(1)}, bf16[8192,64]{1,0:T(8,128)(2,1)}, u32[]{:S(2)}) copy-start(bf16[8192,64]{1,0:T(8,128)(2,1)} %get-tuple-element.341) | copy-start | bytes 3145732 | tf_op jit(solution)/shard_map/while
  972.2 43.4 %copy-start.1 = (bf16[8192,64]{1,0:T(8,128)(2,1)S(1)}, bf16[8192,64]{1,0:T(8,128)(2,1)}, u32[]{:S(2)}) copy-start(bf16[8192,64]{1,0:T(8,128)(2,1)} %get-tuple-element.341) | copy-start | bytes 3145732 | tf_op jit(solution)/shard_map/while
  1066.1 43.4 %copy-start.1 = (bf16[8192,64]{1,0:T(8,128)(2,1)S(1)}, bf16[8192,64]{1,0:T(8,128)(2,1)}, u32[]{:S(2)}) copy-start(bf16[8192,64]{1,0:T(8,128)(2,1)} %get-tuple-element.341) | copy-start | bytes 3145732 | tf_op jit(solution)/shard_map/while
  1160.1 43.4 %copy-start.1 = (bf16[8192,64]{1,0:T(8,128)(2,1)S(1)}, bf16[8192,64]{1,0:T(8,128)(2,1)}, u32[]{:S(2)}) copy-start(bf16[8192,64]{1,0:T(8,128)(2,1)} %get-tuple-element.341) | copy-start | bytes 3145732 | tf_op jit(solution)/shard_map/while
  1254.1 43.4 %copy-start.1 = (bf16[8192,64]{1,0:T(8,128)(2,1)S(1)}, bf16[8192,64]{1,0:T(8,128)(2,1)}, u32[]{:S(2)}) copy-start(bf16[8192,64]{1,0:T(8,128)(2,1)} %get-tuple-element.341) | copy-start | bytes 3145732 | tf_op jit(solution)/shard_map/while
  1348.0 43.4 %copy-start.1 = (bf16[8192,64]{1,0:T(8,128)(2,1)S(1)}, bf16[8192,64]{1,0:T(8,128)(2,1)}, u32[]{:S(2)}) copy-start(bf16[8192,64]{1,0:T(8,128)(2,1)} %get-tuple-element.341) | copy-start | bytes 3145732 | tf_op jit(solution)/shard_map/while
  1442.0 43.4 %copy-start.1 = (bf16[8192,64]{1,0:T(8,128)(2,1)S(1)}, bf16[8192,64]{1,0:T(8,128)(2,1)}, u32[]{:S(2)}) copy-start(bf16[8192,64]{1,0:T(8,128)(2,1)} %get-tuple-element.341) | copy-start | bytes 3145732 | tf_op jit(solution)/shard_map/while
  1536.0 43.4 %copy-start.1 = (bf16[8192,64]{1,0:T(8,128)(2,1)S(1)}, bf16[8192,64]{1,0:T(8,128)(2,1)}, u32[]{:S(2)}) copy-start(bf16[8192,64]{1,0:T(8,128)(2,1)} %get-tuple-element.341) | copy-start | bytes 3145732 | tf_op jit(solution)/shard_map/while
  1581.8 2.5 copy-start.5
  1581.8 2.5 copy-start.6
  1581.8 2.8 copy-start.7
  1581.8 71.7 %copy-start.2 = (bf16[1024,64]{0,1:T(8,128)(2,1)S(1)}, bf16[1024,64]{0,1:T(8,128)(2,1)}, u32[]{:S(2)}) copy-start(bf16[1024,64]{0,1:T(8,128)(2,1)} %param.14) | copy-start | bytes 393220
  1581.8 71.7 %copy-start.3 = (bf16[1024,64]{0,1:T(8,128)(2,1)S(1)}, bf16[1024,64]{0,1:T(8,128)(2,1)}, u32[]{:S(2)}) copy-start(bf16[1024,64]{0,1:T(8,128)(2,1)} %param.15) | copy-start | bytes 393220
  1583.5 70.0 %reduce-scatter.6.cloned.1.call-start = ((), (), s32[]{:S(2)}) async-start(), calls=%async_computation.5 | async-start | bytes 2359296 | tf_op jit(solution)/shard_map/reduce_scatter | solution.py:76
  1584.2 170.4 %reduce-scatter.8.cloned.1.call-start = ((), (), s32[]{:S(2)}) async-start(), calls=%async_computation.6 | async-start | bytes 147456 | tf_op jit(solution)/shard_map/reduce_scatter | solution.py:97
  1654.6 119.9 %copy-start.4 = (f32[1024]{0:T(1024)}, f32[1024]{0:T(1024)S(1)}, u32[]{:S(2)}) copy-start(f32[1024]{0:T(1024)S(1)} %add_reduce_fusion) | copy-start | bytes 12292
Sparse Core Ops, SparseCore 0:
  9.9 30.4 all-gather.1
  1583.6 26.9 reduce-scatter.3
  1613.9 39.5 reduce-scatter.5
  1723.7 30.8 reduce-scatter.7
where the time goes:
time: 1780 us
  matrix products  770 us (43%)
  other arithmetic  698 us (39%)
  blocking collectives  157 us (9%)
  waiting for transfers between devices  100 us (6%)
  local copies, waits for them, and re-layouts  29.5 us (2%)
    dot_general x16, matrix products, advance(): lax.dot_general(tile, adj_rows, (((0,), (0,)), ((), ())), preferred_eleme...  746 us
    dot_general x16, other arithmetic, advance(): image_rows = jnp.dot(tile, dir_src, preferred_element_type=jnp.float32)  694 us
    all_gather x1, blocking collectives, on_device(): lax.all_gather(densities, ('row', 'col'), axis=0, tiled=True)  67.8 us
    reduce_scatter x1, waiting for transfers between devices, on_device(): lax.psum_scatter(adj_part, 'row', scatter_dimension=0, tiled=True)  42.9 us
  transfers between devices with their start and end apart: 4, of which 3 were waited for; matrix products, arithmetic and copies ran while one was open for 0% of the time, Pallas kernels for 0%

commit v1 on v0

v1 whole, which is shorter than its diff:
```python
import functools
import math

import jax
import jax.numpy as jnp
from jax import lax
from jax.experimental import pallas as pl
from jax.experimental.pallas import tpu as pltpu
from jax.sharding import PartitionSpec as P

BPAN = 256
NPATCH = 64
NBLK = 128

wave_number = 6.0
inv_four_pi = 0.07957747154594767

HALF_ANGLE = (
    0.5624999387637301,
    -0.026367050589663217,
    0.0004942961270241117,
    -4.941951390951122e-06,
    2.8141817781696455e-08,
)
SQ_SCALE = HALF_ANGLE[-1] ** (1.0 / len(HALF_ANGLE))
MONIC = tuple(c / SQ_SCALE ** (i + 1) for i, c in enumerate(HALF_ANGLE[:-1]))

T_FIELDS = 7
S_FIELDS = 8


def pair_kernel(step_rows, tgt_ref, src_ref, adj_ref, dir_ref, image_ref, adjoint_ref, tile_ref):
    j = pl.program_id(0)
    i = pl.program_id(1)
    rows_here, lanes_here = tile_ref.shape
    for start in range(0, rows_here, step_rows):
        rows = pl.ds(start, step_rows)

        def column(field):
            return tgt_ref[rows, field : field + 1]

        def row(field):
            full = src_ref[8 * field : 8 * field + 8, :]
            return jnp.concatenate([full] * (step_rows // 8), axis=0)

        tx, ty, tz, nx, ny, nz, tw = [column(f) for f in range(T_FIELDS)]
        sx, sy, sz, sz4, sz2, sa, se, sk = [row(f) for f in range(S_FIELDS)]
        delta_x = tx - sx
        delta_y = ty - sy
        delta_z = tz - sz
        level = delta_x * delta_x + delta_y * delta_y + sa
        near = level + delta_z * delta_z
        mirror = near + tz * sz4
        r_near = lax.rsqrt(near)
        r_mirror = lax.rsqrt(mirror)
        facing = nx * delta_x + ny * delta_y + nz * delta_z
        facing_mirror = facing + nz * sz2
        arc = level + MONIC[3]
        arc = arc * level + MONIC[2]
        arc = arc * level + MONIC[1]
        arc = arc * level + MONIC[0]
        arc = arc * level
        arc = arc * (4.0 - arc)
        arc = arc * (4.0 - arc)
        arc = arc * (4.0 - arc)
        total = (
            facing * (r_near * r_near * r_near)
            + facing_mirror * (r_mirror * r_mirror * r_mirror)
            + (arc - 2.0) * (tw * se)
        )
        tile_ref[rows, :] = (total * sk).astype(jnp.bfloat16)

    tile = tile_ref[...]
    image = jnp.dot(tile, dir_ref[...], preferred_element_type=jnp.float32)
    back = jnp.dot(adj_ref[...], tile, preferred_element_type=jnp.float32)
    out_rows = pl.ds(pl.multiple_of(i * rows_here, rows_here), rows_here)

    @pl.when(j == 0)
    def _():
        image_ref[out_rows, :] = image

    @pl.when(j > 0)
    def _():
        image_ref[out_rows, :] += image

    @pl.when(i == 0)
    def _():
        adjoint_ref[...] = back

    @pl.when(i > 0)
    def _():
        adjoint_ref[...] += back


def pair_images(tgt, src, adj_cols, dir_src):
    targets = tgt.shape[0]
    sources = src.shape[1]
    columns = dir_src.shape[1]
    rows_here = min(targets, 256)
    lanes_here = min(sources, 512)
    return pl.pallas_call(
        functools.partial(pair_kernel, 16),
        grid=(sources // lanes_here, targets // rows_here),
        in_specs=[
            pl.BlockSpec((rows_here, tgt.shape[1]), lambda j, i: (i, 0)),
            pl.BlockSpec((src.shape[0], lanes_here), lambda j, i: (0, j)),
            pl.BlockSpec((columns, rows_here), lambda j, i: (0, i)),
            pl.BlockSpec((lanes_here, columns), lambda j, i: (j, 0)),
        ],
        out_specs=[
            pl.BlockSpec((targets, columns), lambda j, i: (0, 0)),
            pl.BlockSpec((columns, lanes_here), lambda j, i: (0, j)),
        ],
        out_shape=[
            jax.ShapeDtypeStruct((targets, columns), jnp.float32),
            jax.ShapeDtypeStruct((columns, sources), jnp.float32),
        ],
        scratch_shapes=[pltpu.VMEM((rows_here, lanes_here), jnp.bfloat16)],
        name="pair_images",
    )(tgt, src, adj_cols, dir_src)


def on_device(
    positions, normals, areas, direct, adjoint, spline, block_lists, patch_counts, patch_owner
):
    length = math.sqrt(SQ_SCALE)
    depth = 0.5 * (positions[2] - 1.2)
    grow = jnp.exp(wave_number * depth)
    flat = length * positions[:2]
    deep = (length * depth)[None]
    tgt_fields = jnp.concatenate(
        [
            flat,
            deep,
            normals,
            ((wave_number / SQ_SCALE) * normals[2] * grow)[None],
        ],
        axis=0,
    )
    src_fields = jnp.concatenate(
        [flat, deep, (SQ_SCALE * areas)[None], grow[None], ((SQ_SCALE * inv_four_pi) * areas)[None]],
        axis=0,
    )
    tgt_all = lax.all_gather(tgt_fields, "col", axis=1, tiled=True)
    src_all = lax.all_gather(src_fields, "row", axis=1, tiled=True)
    adj_tgt = lax.all_gather(adjoint, "col", axis=0, tiled=True)
    dir_src = lax.all_gather(direct, "row", axis=0, tiled=True)
    tgt = jnp.pad(tgt_all.T, ((0, 0), (0, 8 - T_FIELDS)))
    sz = src_all[2:3]
    src = jnp.repeat(
        jnp.concatenate([src_all[:3], 4.0 * sz, 2.0 * sz, src_all[3:]], axis=0), 8, axis=0
    )
    image, back = pair_images(tgt, src, adj_tgt.T, dir_src)
    dens_tgt = jnp.sum(adj_tgt.astype(jnp.float32) * image, axis=1)
    dens_src = jnp.sum(dir_src.T.astype(jnp.float32) * back, axis=0)
    densities = lax.psum_scatter(
        dens_tgt, "col", scatter_dimension=0, tiled=True
    ) + lax.psum_scatter(dens_src, "row", scatter_dimension=0, tiled=True)
    every_density = lax.all_gather(densities, ("row", "col"), axis=0, tiled=True)
    blocks = every_density.reshape(NBLK, BPAN)
    ends = jnp.cumsum(patch_counts)
    starts = ends - patch_counts
    block_ids = jnp.arange(NBLK, dtype=jnp.int32)
    inside = (
        (starts[:, None] <= block_ids[None, :]) & (block_ids[None, :] < ends[:, None])
    ).astype(jnp.float32)
    owners = (patch_owner[None, :] == jnp.arange(NPATCH, dtype=jnp.int32)[:, None]).astype(
        jnp.float32
    )
    owned = jnp.dot(owners, inside, precision=lax.Precision.HIGHEST)
    holder = lax.axis_index(("row", "col"))
    listed = jnp.any(block_lists == holder, axis=1).astype(jnp.float32)
    weights = owned * listed[None, :]
    gathered = jnp.dot(weights, blocks, precision=lax.Precision.HIGHEST)
    contrib = jnp.dot(gathered, spline[0].astype(jnp.float32), precision=lax.Precision.HIGHEST)
    partial_rows = lax.psum_scatter(contrib, "row", scatter_dimension=0, tiled=True)
    patch_grad = lax.psum(partial_rows, "col")
    return (densities, patch_grad)


def solution(mesh):
    placed = (
        P(None, ("row", "col")),
        P(None, ("row", "col")),
        P(("row", "col")),
        P(("row", "col"), None),
        P(("row", "col"), None),
        P(("row", "col"), None, None),
        P(),
        P(),
        P(),
    )
    return jax.shard_map(
        on_device,
        mesh=mesh,
        in_specs=placed,
        out_specs=(P(("row", "col")), P("row", None)),
        check_vma=False,
    )
```

time: 1780 us -> 558 us (0.31)
  matrix products: 770 us -> 1.32 us
  other arithmetic: 698 us -> 6.82 us
  Pallas kernels: 0 us -> 296 us
  waiting for transfers between devices: 100 us -> 32.7 us
  blocking collectives: 157 us -> 193 us
    dot_general x32 -> x0, matrix products: 769 us -> none  [the longest x16 746 us: advance(): lax.dot_general(tile, adj_rows, (((0,), (0,)), ((), ())), preferred_eleme...]
    dot_general x16 -> x0, other arithmetic: 694 us -> none  [advance(): image_rows = jnp.dot(tile, dir_src, preferred_element_type=jnp.float32)]
    pallas_call x0 -> x1, Pallas kernels: none -> 296 us  [pair_images(): pl.pallas_call(functools.partial(pair_kernel, 16), grid=(sources // lanes...]
    reduce_scatter x2 -> x0, waiting for transfers between devices: 68.7 us -> none  [the longest x1 42.9 us: on_device(): lax.psum_scatter(adj_part, 'row', scatter_dimension=0, tiled=True)]
    unnamed x0 -> x2, blocking collectives: none -> 42.1 us
    all_gather x4 -> x2, blocking collectives: 46.6 us -> 49.4 us  [the longest x1 38.5 us: on_device(): tgt_all = lax.all_gather(tgt_fields, 'col', axis=1, tiled=True)]
  transfers between devices with their start and end apart: 4 -> 2, of which waited for: 3 -> 1; matrix products, arithmetic and copies ran while one was open for 0% -> 1% of each run, Pallas kernels for 0% -> 0%
where the time goes in v1:
time: 558 us; the launch traced here: 557 us
  Pallas kernels  296 us (53%)
  blocking collectives  193 us (35%)
  waiting for transfers between devices  32.7 us (6%)
  between operations  15.5 us (3%)
  local copies, waits for them, and re-layouts  12.5 us (2%)
  other arithmetic  6.82 us (1%)
    pallas_call x1, Pallas kernels, pair_images(): pl.pallas_call(functools.partial(pair_kernel, 16), grid=(sources // lanes...  296 us
    all_gather x1, blocking collectives, on_device(): lax.all_gather(densities, ('row', 'col'), axis=0, tiled=True)  64.4 us
    unnamed x2, blocking collectives  42.1 us
    all_gather x1, blocking collectives, on_device(): tgt_all = lax.all_gather(tgt_fields, 'col', axis=1, tiled=True)  38.5 us
    reduce_scatter x1, waiting for transfers between devices, on_device(): lax.psum_scatter(contrib, 'row', scatter_dimension=0, tiled=True)  32.7 us
    psum x1, blocking collectives, on_device(): patch_grad = lax.psum(partial_rows, 'col')  19.9 us
    all_gather x1, blocking collectives, on_device(): adj_tgt = lax.all_gather(adjoint, 'col', axis=0, tiled=True)  17 us
  transfers between devices with their start and end apart: 2, of which 1 were waited for; matrix products, arithmetic and copies ran while one was open for 1% of the time, Pallas kernels for 0%

profile of v1, /device:TPU:0, one launch (start us, length us, event | category | flops | bytes accessed | tf_op | source)
XLA Modules:
  0.0 557.4 jit_solution(7532264662019065853)
XLA Ops:
  7.2 0.0 copy-start
  7.2 0.0 all-gather.2.cloned.1.call-start
  7.2 1.8 copy.40
  9.0 0.0 all-gather.2.cloned.1.call-update
  9.0 0.0 reduce-scatter.2.cloned.1.call-start
  9.1 0.7 slice_multiply_fusion.2
  9.8 0.8 multiply_multiply_fusion
  10.6 0.7 broadcast_multiply_fusion
  11.3 0.0 copy-start.3
  11.3 10.9 %all_gather.17 = f32[6,8192]{1,0:T(8,128)S(1)} all-gather(f32[6,1024]{1,0:T(8,128)S(1)} %concatenate.10), channel_id=1, replica_groups=mesh['row'=8,'col'=4] {'row'}, dimensions={1}, use_global_device_ids=true | all-gather | bytes 221184 | tf_op jit(solution)/shard_map/all_gather | solution.py:145
  22.2 0.1 fusion.8
  22.3 0.0 copy-start.9
  22.3 0.0 copy-start.8
  22.3 0.0 copy-start.5
  22.3 0.0 copy-start.6
  22.3 0.1 slice_multiply_fusion.1
  22.4 0.7 pad_maximum_fusion.1
  23.2 0.2 copy.39
  23.4 38.5 %all_gather.16 = f32[7,4096]{0,1:T(8,128)S(1)} all-gather(f32[7,1024]{0,1:T(8,128)S(1)} %copy.39), channel_id=1, replica_groups=mesh['row'=8,'col'=4] {'col'}, dimensions={1}, use_global_device_ids=true | all-gather | bytes 143360 | tf_op jit(solution)/shard_map/all_gather | solution.py:144
  61.9 0.0 copy-done.3
  61.9 17.0 %all_gather.15 = bf16[4096,64]{0,1:T(8,128)(2,1)} all-gather(bf16[1024,64]{0,1:T(8,128)(2,1)S(1)} %copy-done.3), channel_id=1, replica_groups=mesh['row'=8,'col'=4] {'col'}, dimensions={0}, use_global_device_ids=true | all-gather | bytes 655360 | tf_op jit(solution)/shard_map/all_gather | solution.py:146
  78.9 0.0 copy-done.9
  78.9 0.6 dynamic-slice
  79.5 0.0 copy-done.8
  79.5 0.6 dynamic-slice.2
  81.4 0.0 copy-done.5
  81.4 0.0 copy-done.6
  81.4 0.1 copy.43
  81.5 0.1 reduce-window.8
  81.6 0.1 reduce
  81.7 0.0 copy-start.7
  81.8 1.5 pad.4.tgt_ref
  83.3 0.0 copy-done.7
  83.3 0.2 convolution_multiply_fusion
  83.5 0.1 pad_maximum_fusion
  83.6 1.4 broadcast_bitcast_fusion.src_ref
  85.0 0.0 all-gather.2.cloned.1.call-done.dir_ref
  85.0 295.6 %pair_images.1 = (f32[4096,64]{1,0:T(8,128)}, f32[64,8192]{1,0:T(8,128)}) custom-call(f32[4096,8]{1,0:T(8,128)} %pad.4.tgt_ref, f32[64,8192]{1,0:T(8,128)} %broadcast_bitcast_fusion.src_ref, bf16[64,4096]{1,0:T(8,128)(2,1)} %bitcast.20, bf16[8192,64]{1,0:T(8,128)(2,1)} %all-gather.2.cloned.1.call-done.dir_ref), custom_call_target="tpu_custom_call" | custom-call | tf_op jit(solution)/shard_map/pair_images/pallas_call | solution.py:101
  380.6 0.0 copy-start.1
  380.6 3.9 copy.42
  384.6 0.0 copy-done.1
  384.6 3.3 fusion
  387.9 0.0 copy-start.2
  387.9 22.5 %all-reduce.2 = f32[8192]{0:T(1024)S(1)} all-reduce(f32[8192]{0:T(1024)S(1)} %fusion), channel_id=3, replica_groups=mesh['row'=8,'col'=4] {'row'}, use_global_device_ids=true, to_apply=%region_3.4.clone | all-reduce | flops 8192 | bytes 65536
  410.4 2.2 copy.41
  412.6 0.0 copy-done.2
  412.6 0.1 multiply_reduce_fusion
  412.7 19.6 %all-reduce.1 = f32[4096]{0:T(1024)S(1)} all-reduce(f32[4096]{0:T(1024)S(1)} %multiply_reduce_fusion), channel_id=2, replica_groups=mesh['row'=8,'col'=4] {'col'}, use_global_device_ids=true, to_apply=%region_1.2.clone | all-reduce | flops 4096 | bytes 32768
  432.4 0.0 copy-start.4
  432.4 64.4 %all_gather.19 = f32[32768]{0:T(1024)S(1)} all-gather(f32[1024]{0:T(1024)S(1)} %dynamic-slice_add_fusion), channel_id=1, replica_groups=mesh['row'=8,'col'=4] {'row','col'}, dimensions={0}, use_global_device_ids=true | all-gather | bytes 135168 | tf_op jit(solution)/shard_map/all_gather | solution.py:159
  496.8 0.2 fusion.9
  497.0 0.0 copy-done
  497.0 0.9 fusion.1
  497.9 0.0 reduce-scatter.2.cloned.1.call-update
  497.9 32.7 %reduce-scatter.2.cloned.1.call-done = f32[8,512]{1,0:T(8,128)} async-done(((f32[64,512]{1,0:T(8,128)}), f32[8,512]{1,0:T(8,128)}) %reduce-scatter.2.cloned.1.call-update) | async-done | bytes 16400 | tf_op jit(solution)/shard_map/reduce_scatter | solution.py:176
  530.6 19.9 %psum.7 = f32[8,512]{1,0:T(8,128)} all-reduce(f32[8,512]{1,0:T(8,128)} %reduce-scatter.2.cloned.1.call-done), channel_id=1, replica_groups=mesh['row'=8,'col'=4] {'col'}, use_global_device_ids=true, to_apply=%region_7.8 | all-reduce | flops 4096 | bytes 32768 | tf_op jit(solution)/shard_map/psum | solution.py:177
  550.5 0.0 copy-done.4
  (6 shorter events, 0.1 us)
Async XLA Ops:
  7.2 489.8 %copy-start = (bf16[1,256,512]{2,1,0:T(8,128)(2,1)S(1)}, bf16[1,256,512]{2,1,0:T(8,128)(2,1)}, u32[]{:S(2)}) copy-start(bf16[1,256,512]{2,1,0:T(8,128)(2,1)} %param.14) | copy-start | bytes 786436
  7.2 77.8 %all-gather.2.cloned.1.call-start = ((), (), s32[]{:S(2)}) async-start(), calls=%async_computation.1 | async-start | bytes 2359296 | tf_op jit(solution)/shard_map/all_gather | solution.py:147
  9.0 521.6 %reduce-scatter.2.cloned.1.call-start = ((), (), s32[]{:S(2)}) async-start(), calls=%async_computation.2 | async-start | bytes 147456 | tf_op jit(solution)/shard_map/reduce_scatter | solution.py:176
  11.3 50.6 %copy-start.3 = (bf16[1024,64]{0,1:T(8,128)(2,1)S(1)}, bf16[1024,64]{0,1:T(8,128)(2,1)}, u32[]{:S(2)}) copy-start(bf16[1024,64]{0,1:T(8,128)(2,1)} %param.13) | copy-start | bytes 393220
  22.3 56.6 %copy-start.9 = (u32[32]{0:T(128)S(1)}, u32[32]{0:T(128)}, u32[]{:S(2)}) copy-start(u32[32]{0:T(128)} %constant.48) | copy-start | bytes 388
  22.3 57.2 %copy-start.8 = (u32[32]{0:T(128)S(1)}, u32[32]{0:T(128)}, u32[]{:S(2)}) copy-start(u32[32]{0:T(128)} %constant.52) | copy-start | bytes 388
  22.3 59.1 %copy-start.5 = (s32[128,4]{0,1:T(4,128)S(1)}, s32[128,4]{0,1:T(4,128)}, u32[]{:S(2)}) copy-start(s32[128,4]{0,1:T(4,128)} %param.15) | copy-start | bytes 6148
  22.3 59.1 %copy-start.6 = (s32[64]{0:T(128)S(1)}, s32[64]{0:T(128)}, u32[]{:S(2)}) copy-start(s32[64]{0:T(128)} %param.16) | copy-start | bytes 772
  81.7 1.5 copy-start.7
  380.6 3.9 copy-start.1
  387.9 24.7 %copy-start.2 = (bf16[4096,64]{0,1:T(8,128)(2,1)S(1)}, bf16[4096,64]{0,1:T(8,128)(2,1)}, u32[]{:S(2)}) copy-start(bf16[4096,64]{0,1:T(8,128)(2,1)} %all_gather.15) | copy-start | bytes 1572868
  432.4 118.2 %copy-start.4 = (f32[1024]{0:T(1024)}, f32[1024]{0:T(1024)S(1)}, u32[]{:S(2)}) copy-start(f32[1024]{0:T(1024)S(1)} %dynamic-slice_add_fusion) | copy-start | bytes 12292
Sparse Core Ops, SparseCore 0:
  9.9 30.4 all-gather.1
  498.0 32.4 reduce-scatter.1

commit v2 on v1

--- a/solution.py
+++ b/solution.py
@@ -71,7 +71,9 @@
         tile_ref[rows, :] = (total * sk).astype(jnp.bfloat16)
 
     tile = tile_ref[...]
-    image = jnp.dot(tile, dir_ref[...], preferred_element_type=jnp.float32)
+    image = lax.dot_general(
+        tile, dir_ref[...], (((1,), (1,)), ((), ())), preferred_element_type=jnp.float32
+    )
     back = jnp.dot(adj_ref[...], tile, preferred_element_type=jnp.float32)
     out_rows = pl.ds(pl.multiple_of(i * rows_here, rows_here), rows_here)
 
@@ -92,11 +94,11 @@
         adjoint_ref[...] += back
 
 
-def pair_images(tgt, src, adj_cols, dir_src):
+def pair_images(tgt, src, adj_cols, dir_cols):
     targets = tgt.shape[0]
     sources = src.shape[1]
-    columns = dir_src.shape[1]
-    rows_here = min(targets, 256)
+    columns = dir_cols.shape[0]
+    rows_here = min(targets, 512)
     lanes_here = min(sources, 512)
     return pl.pallas_call(
         functools.partial(pair_kernel, 16),
@@ -105,7 +107,7 @@
             pl.BlockSpec((rows_here, tgt.shape[1]), lambda j, i: (i, 0)),
             pl.BlockSpec((src.shape[0], lanes_here), lambda j, i: (0, j)),
             pl.BlockSpec((columns, rows_here), lambda j, i: (0, i)),
-            pl.BlockSpec((lanes_here, columns), lambda j, i: (j, 0)),
+            pl.BlockSpec((columns, lanes_here), lambda j, i: (0, j)),
         ],
         out_specs=[
             pl.BlockSpec((targets, columns), lambda j, i: (0, 0)),
@@ -117,46 +119,265 @@
         ],
         scratch_shapes=[pltpu.VMEM((rows_here, lanes_here), jnp.bfloat16)],
         name="pair_images",
-    )(tgt, src, adj_cols, dir_src)
+    )(tgt, src, adj_cols, dir_cols)
+
+
+MESH = pl.DeviceIdType.MESH
+
+
+def others(nrow, ncol):
+    r, c = lax.axis_index("row"), lax.axis_index("col")
+    along_col = [(r, lax.rem(c + k, ncol)) for k in range(1, ncol)]
+    along_row = [(lax.rem(r + k, nrow), c) for k in range(1, nrow)]
+    return r, c, along_col, along_row
+
+
+def greet(peers):
+    barrier = pltpu.get_barrier_semaphore()
+    for peer in peers:
+        pl.semaphore_signal(barrier, inc=1, device_id=peer, device_id_type=MESH)
+    pl.semaphore_wait(barrier, len(peers))
+
+
+def send(source, target, send_sem, recv_sem, slot, peer):
+    copy = pltpu.make_async_remote_copy(
+        src_ref=source,
+        dst_ref=target,
+        send_sem=send_sem.at[slot],
+        recv_sem=recv_sem.at[slot],
+        device_id=peer,
+        device_id_type=MESH,
+    )
+    copy.start()
+    return copy
+
+
+def gather_kernel(
+    nrow,
+    ncol,
+    tgt_ref,
+    adj_ref,
+    src_ref,
+    dir_ref,
+    tgt_all,
+    adj_all,
+    src_all,
+    dir_all,
+    send_sem,
+    recv_sem,
+    own_sem,
+):
+    r, c, along_col, along_row = others(nrow, ncol)
+    greet(along_col + along_row)
+    copies = []
+    for peer in along_row:
+        for source, target in ((dir_ref, dir_all), (src_ref, src_all)):
+            copies.append(send(source, target.at[r], send_sem, recv_sem, len(copies), peer))
+    for peer in along_col:
+        for source, target in ((adj_ref, adj_all), (tgt_ref, tgt_all)):
+            copies.append(send(source, target.at[c], send_sem, recv_sem, len(copies), peer))
+    mine = (
+        (tgt_ref, tgt_all.at[c]),
+        (adj_ref, adj_all.at[c]),
+        (src_ref, src_all.at[r]),
+        (dir_ref, dir_all.at[r]),
+    )
+    kept = []
+    for slot, (source, target) in enumerate(mine):
+        copy = pltpu.make_async_copy(source, target, own_sem.at[slot])
+        copy.start()
+        kept.append(copy)
+    for copy in kept + copies:
+        copy.wait()
+
+
+def gather_all(nrow, ncol, tgt, adj, src, direct):
+    count = 2 * (nrow + ncol - 2)
+    anywhere = pl.BlockSpec(memory_space=pl.ANY)
+    return pl.pallas_call(
+        functools.partial(gather_kernel, nrow, ncol),
+        in_specs=[anywhere] * 4,
+        out_specs=[anywhere] * 4,
+        out_shape=[
+            jax.ShapeDtypeStruct((number,) + x.shape, x.dtype)
+            for number, x in ((ncol, tgt), (ncol, adj), (nrow, src), (nrow, direct))
+        ],
+        scratch_shapes=[
+            pltpu.SemaphoreType.DMA((count,)),
+            pltpu.SemaphoreType.DMA((count,)),
+            pltpu.SemaphoreType.DMA((4,)),
+        ],
+        compiler_params=pltpu.CompilerParams(collective_id=0, has_side_effects=True),
+        name="gather_all",
+    )(tgt, adj, src, direct)
+
+
+def density_kernel(
+    nrow, ncol, tgt_ref, src_ref, mine_ref, every_ref, got_tgt, got_src, send_sem, recv_sem
+):
+    r, c, along_col, along_row = others(nrow, ncol)
+    greet(along_col + along_row)
+    copies = []
+    for k, peer in enumerate(along_col):
+        copies.append(
+            send(tgt_ref.at[peer[1]], got_tgt.at[k], send_sem, recv_sem, len(copies), peer)
+        )
+    for k, peer in enumerate(along_row):
+        copies.append(
+            send(src_ref.at[peer[0]], got_src.at[k], send_sem, recv_sem, len(copies), peer)
+        )
+    total = tgt_ref[c] + src_ref[r]
+    for copy in copies:
+        copy.wait()
+    for k in range(ncol - 1):
+        total = total + got_tgt[k]
+    for k in range(nrow - 1):
+        total = total + got_src[k]
+    mine_ref[...] = total
+    every_ref[r, c] = total
+    first = len(copies)
+    spread = [
+        send(every_ref.at[r, c], every_ref.at[r, c], send_sem, recv_sem, first + k, peer)
+        for k, peer in enumerate(along_col)
+    ]
+    for copy in spread:
+        copy.wait()
+    first = first + len(spread)
+    spread = [
+        send(every_ref.at[r], every_ref.at[r], send_sem, recv_sem, first + k, peer)
+        for k, peer in enumerate(along_row)
+    ]
+    for copy in spread:
+        copy.wait()
+
+
+def sum_densities(nrow, ncol, tgt, src):
+    size = tgt.shape[-1]
+    count = 2 * (nrow + ncol - 2)
+    vmem = pl.BlockSpec(memory_space=pltpu.VMEM)
+    return pl.pallas_call(
+        functools.partial(density_kernel, nrow, ncol),
+        in_specs=[vmem] * 2,
+        out_specs=[vmem] * 2,
+        out_shape=[
+            jax.ShapeDtypeStruct((1, size), jnp.float32),
+            jax.ShapeDtypeStruct((nrow, ncol, 1, size), jnp.float32),
+        ],
+        scratch_shapes=[
+            pltpu.VMEM((ncol - 1, 1, size), jnp.float32),
+            pltpu.VMEM((nrow - 1, 1, size), jnp.float32),
+            pltpu.SemaphoreType.DMA((count,)),
+            pltpu.SemaphoreType.DMA((count,)),
+        ],
+        compiler_params=pltpu.CompilerParams(collective_id=1, has_side_effects=True),
+        name="sum_densities",
+    )(tgt, src)
+
+
+def patch_kernel(nrow, ncol, part_ref, out_ref, got, sums, send_sem, recv_sem):
+    r, c, along_col, along_row = others(nrow, ncol)
+    greet(along_col + along_row)
+    copies = [
+        send(part_ref.at[peer[0]], got.at[k], send_sem, recv_sem, k, peer)
+        for k, peer in enumerate(along_row)
+    ]
+    total = part_ref[r]
+    for copy in copies:
+        copy.wait()
+    for k in range(nrow - 1):
+        total = total + got[k]
+    sums[c] = total
+    first = len(copies)
+    copies = [
+        send(sums.at[c], sums.at[c], send_sem, recv_sem, first + k, peer)
+        for k, peer in enumerate(along_col)
+    ]
+    for copy in copies:
+        copy.wait()
+    total = sums[0]
+    for k in range(1, ncol):
+        total = total + sums[k]
+    out_ref[...] = total
+
+
+def sum_patches(nrow, ncol, part):
+    count = nrow + ncol - 2
+    vmem = pl.BlockSpec(memory_space=pltpu.VMEM)
+    return pl.pallas_call(
+        functools.partial(patch_kernel, nrow, ncol),
+        in_specs=[vmem],
+        out_specs=vmem,
+        out_shape=jax.ShapeDtypeStruct(part.shape[1:], jnp.float32),
+        scratch_shapes=[
+            pltpu.VMEM((nrow - 1,) + part.shape[1:], jnp.float32),
+            pltpu.VMEM((ncol,) + part.shape[1:], jnp.float32),
+            pltpu.SemaphoreType.DMA((count,)),
+            pltpu.SemaphoreType.DMA((count,)),
+        ],
+        compiler_params=pltpu.CompilerParams(collective_id=2, has_side_effects=True),
+        name="sum_patches",
+    )(part)
 
 
 def on_device(
-    positions, normals, areas, direct, adjoint, spline, block_lists, patch_counts, patch_owner
+    nrow,
+    ncol,
+    positions,
+    normals,
+    areas,
+    direct,
+    adjoint,
+    spline,
+    block_lists,
+    patch_counts,
+    patch_owner,
 ):
     length = math.sqrt(SQ_SCALE)
     depth = 0.5 * (positions[2] - 1.2)
     grow = jnp.exp(wave_number * depth)
     flat = length * positions[:2]
     deep = (length * depth)[None]
+    size = positions.shape[1]
     tgt_fields = jnp.concatenate(
         [
             flat,
             deep,
             normals,
             ((wave_number / SQ_SCALE) * normals[2] * grow)[None],
+            jnp.zeros_like(deep),
         ],
         axis=0,
     )
     src_fields = jnp.concatenate(
-        [flat, deep, (SQ_SCALE * areas)[None], grow[None], ((SQ_SCALE * inv_four_pi) * areas)[None]],
+        [
+            flat,
+            deep,
+            4.0 * deep,
+            2.0 * deep,
+            (SQ_SCALE * areas)[None],
+            grow[None],
+            ((SQ_SCALE * inv_four_pi) * areas)[None],
+        ],
         axis=0,
     )
-    tgt_all = lax.all_gather(tgt_fields, "col", axis=1, tiled=True)
-    src_all = lax.all_gather(src_fields, "row", axis=1, tiled=True)
-    adj_tgt = lax.all_gather(adjoint, "col", axis=0, tiled=True)
-    dir_src = lax.all_gather(direct, "row", axis=0, tiled=True)
-    tgt = jnp.pad(tgt_all.T, ((0, 0), (0, 8 - T_FIELDS)))
-    sz = src_all[2:3]
-    src = jnp.repeat(
-        jnp.concatenate([src_all[:3], 4.0 * sz, 2.0 * sz, src_all[3:]], axis=0), 8, axis=0
-    )
-    image, back = pair_images(tgt, src, adj_tgt.T, dir_src)
-    dens_tgt = jnp.sum(adj_tgt.astype(jnp.float32) * image, axis=1)
-    dens_src = jnp.sum(dir_src.T.astype(jnp.float32) * back, axis=0)
-    densities = lax.psum_scatter(
-        dens_tgt, "col", scatter_dimension=0, tiled=True
-    ) + lax.psum_scatter(dens_src, "row", scatter_dimension=0, tiled=True)
-    every_density = lax.all_gather(densities, ("row", "col"), axis=0, tiled=True)
+    tgt_all, adj_all, src_all, dir_all = gather_all(
+        nrow, ncol, tgt_fields, adjoint.T, src_fields, direct.T
+    )
+
+    def beside(chunks):
+        return jnp.swapaxes(chunks, 0, 1).reshape(chunks.shape[1], -1)
+
+    tgt = jnp.swapaxes(tgt_all, 1, 2).reshape(-1, tgt_all.shape[1])
+    src = jnp.repeat(beside(src_all), 8, axis=0)
+    adj_cols = beside(adj_all)
+    dir_cols = beside(dir_all)
+    image, back = pair_images(tgt, src, adj_cols, dir_cols)
+    dens_tgt = jnp.sum(adj_cols.astype(jnp.float32) * image.T, axis=0)
+    dens_src = jnp.sum(dir_cols.astype(jnp.float32) * back, axis=0)
+    densities, every_density = sum_densities(
+        nrow, ncol, dens_tgt.reshape(ncol, 1, size), dens_src.reshape(nrow, 1, size)
+    )
+    densities = densities.reshape(size)
     blocks = every_density.reshape(NBLK, BPAN)
     ends = jnp.cumsum(patch_counts)
     starts = ends - patch_counts
@@ -173,8 +394,7 @@
     weights = owned * listed[None, :]
     gathered = jnp.dot(weights, blocks, precision=lax.Precision.HIGHEST)
     contrib = jnp.dot(gathered, spline[0].astype(jnp.float32), precision=lax.Precision.HIGHEST)
-    partial_rows = lax.psum_scatter(contrib, "row", scatter_dimension=0, tiled=True)
-    patch_grad = lax.psum(partial_rows, "col")
+    patch_grad = sum_patches(nrow, ncol, contrib.reshape(nrow, -1, contrib.shape[1]))
     return (densities, patch_grad)
 
 
@@ -191,7 +411,7 @@
         P(),
     )
     return jax.shard_map(
-        on_device,
+        functools.partial(on_device, mesh.shape["row"], mesh.shape["col"]),
         mesh=mesh,
         in_specs=placed,
         out_specs=(P(("row", "col")), P("row", None)),

time: 558 us -> 345 us (0.62)
  blocking collectives: 193 us -> 0 us
  waiting for transfers between devices: 32.7 us -> 0 us
  Pallas kernels: 296 us -> 321 us
  between operations: 15.5 us -> 0.78 us
    all_gather x4 -> x0, blocking collectives: 131 us -> none  [the longest x1 64.4 us: on_device(): lax.all_gather(densities, ('row', 'col'), axis=0, tiled=True)]
    pallas_call x0 -> x3, Pallas kernels: none -> 46.4 us  [the longest x1 19.9 us: gather_all(): pl.pallas_call(functools.partial(gather_kernel, nrow, ncol), in_specs=[an...]
    unnamed x2 -> x0, blocking collectives: 42.1 us -> none
    reduce_scatter x1 -> x0, waiting for transfers between devices: 32.7 us -> none  [on_device(): lax.psum_scatter(contrib, 'row', scatter_dimension=0, tiled=True)]
    pallas_call x1, Pallas kernels: 296 us -> 275 us  [pair_images(): pl.pallas_call(functools.partial(pair_kernel, 16), grid=(sources // lanes...]
    psum x1 -> x0, blocking collectives: 19.9 us -> none  [on_device(): patch_grad = lax.psum(partial_rows, 'col')]
  transfers between devices with their start and end apart: 2 -> 0, of which waited for: 1 -> 0; matrix products, arithmetic and copies ran while one was open for 1% -> 0% of each run, Pallas kernels for 0% -> 0%
where the time goes in v2:
time: 345 us; the launch traced here: 344 us
  Pallas kernels  321 us (93%)
  local copies, waits for them, and re-layouts  13.7 us (4%)
  other arithmetic  6.91 us (2%)
    pallas_call x1, Pallas kernels, pair_images(): pl.pallas_call(functools.partial(pair_kernel, 16), grid=(sources // lanes...  275 us
    pallas_call x1, Pallas kernels, gather_all(): pl.pallas_call(functools.partial(gather_kernel, nrow, ncol), in_specs=[an...  19.9 us
    pallas_call x1, Pallas kernels, sum_densities(): pl.pallas_call(functools.partial(density_kernel, nrow, ncol), in_specs=[v...  16.3 us
    pallas_call x1, Pallas kernels, sum_patches(): pl.pallas_call(functools.partial(patch_kernel, nrow, ncol), in_specs=[vme...  10.2 us

profile of v2, /device:TPU:0, one launch (start us, length us, event | category | flops | bytes accessed | tf_op | source)
XLA Modules:
  0.0 343.9 jit_solution(4951938973366203232)
XLA Ops:
  0.6 0.0 copy-start
  0.6 0.8 multiply_exponential_fusion
  1.5 0.7 broadcast_multiply_fusion
  2.1 0.7 slice_multiply_fusion
  2.9 0.6 concatenate.7.src_ref
  3.5 1.3 concatenate.6.tgt_ref
  4.9 19.9 %gather_all.1 = (f32[4,8,1024]{2,1,0:T(8,128)}, bf16[4,64,1024]{2,1,0:T(8,128)(2,1)}, f32[8,8,1024]{2,1,0:T(8,128)}, bf16[8,64,1024]{2,1,0:T(8,128)(2,1)}) custom-call(f32[8,1024]{1,0:T(8,128)} %concatenate.6.tgt_ref, bf16[64,1024]{1,0:T(8,128)(2,1)} %bitcast.44, f32[8,1024]{1,0:T(8,128)} %concatenate.7.src_ref, bf16[64,1024]{1,0:T(8,128)(2,1)} %bitcast.45), custom_call_target="tpu_custom_call" | custom-call | tf_op jit(solution)/shard_map/gather_all/pallas_call | solution.py:197
  24.8 0.0 copy-start.3
  24.8 0.0 copy-start.5
  24.8 2.4 copy.22
  27.2 0.0 copy-start.4
  27.2 0.0 copy-done.3
  27.2 0.8 copy.21
  28.1 0.0 copy-done.5
  28.1 1.9 copy.17
  30.0 0.0 copy-done.4
  30.0 1.5 broadcast_bitcast_fusion.src_ref
  31.5 0.0 copy-start.1
  31.5 274.7 %pair_images.1 = (f32[4096,64]{1,0:T(8,128)}, f32[64,8192]{1,0:T(8,128)}) custom-call(f32[4096,8]{1,0:T(8,128)} %bitcast.36, f32[64,8192]{1,0:T(8,128)} %broadcast_bitcast_fusion.src_ref, bf16[64,4096]{1,0:T(8,128)(2,1)} %bitcast.37, bf16[64,8192]{1,0:T(8,128)(2,1)} %bitcast.34), custom_call_target="tpu_custom_call" | custom-call | tf_op jit(solution)/shard_map/pair_images/pallas_call | solution.py:103
  306.2 0.0 copy-done.1
  306.2 2.5 multiply_reduce_fusion
  308.7 0.0 copy-start.2
  308.7 0.0 copy-start.6
  308.7 0.0 copy-start.7
  308.7 0.0 copy-start.8
  308.7 2.2 copy.19
  310.9 0.0 copy-done.2
  311.0 0.7 fusion.1
  311.7 16.3 %sum_densities.1 = (f32[1,1024]{1,0:T(1,128)}, f32[8,4,1,1024]{3,2,1,0:T(1,128)}) custom-call(f32[4,1,1024]{2,1,0:T(1,128)} %bitcast.46, f32[8,1,1024]{2,1,0:T(1,128)} %bitcast.42), custom_call_target="tpu_custom_call" | custom-call | tf_op jit(solution)/shard_map/sum_densities/pallas_call | solution.py:258
  328.1 1.2 reduce.1
  329.3 0.1 reshape.74
  329.4 0.0 copy-done.6
  329.4 0.0 copy-done.7
  329.4 0.1 copy.20
  329.5 0.1 reduce-window.8
  329.6 0.1 reduce
  329.8 0.0 copy-done.8
  329.8 0.2 fusion
  330.0 0.2 fusion.9
  330.2 0.0 copy-done
  330.2 0.9 fusion.2.part_ref
  331.1 10.2 %sum_patches.1 = f32[8,512]{1,0:T(8,128)} custom-call(f32[8,8,512]{2,1,0:T(8,128)} %fusion.2.part_ref), custom_call_target="tpu_custom_call" | custom-call | tf_op jit(solution)/shard_map/sum_patches/pallas_call | solution.py:306
  341.3 1.3 copy.25
  342.6 1.3 copy.26
  (4 shorter events, 0.0 us)
Async XLA Ops:
  0.6 329.6 %copy-start = (bf16[1,256,512]{2,1,0:T(8,128)(2,1)S(1)}, bf16[1,256,512]{2,1,0:T(8,128)(2,1)}, u32[]{:S(2)}) copy-start(bf16[1,256,512]{2,1,0:T(8,128)(2,1)} %param.14) | copy-start | bytes 786436
  24.8 2.5 copy-start.3
  24.8 3.3 copy-start.5
  27.2 2.8 copy-start.4
  31.5 274.8 %copy-start.1 = (bf16[8,8,8,1024]{3,2,0,1:T(8,128)(2,1)S(1)}, bf16[8,8,8,1024]{3,2,0,1:T(8,128)(2,1)}, u32[]{:S(2)}) copy-start(bf16[8,8,8,1024]{3,2,0,1:T(8,128)(2,1)} %copy.22) | copy-start | bytes 3145732
  308.7 2.2 copy-start.2
  308.7 20.7 %copy-start.6 = (s32[128,4]{0,1:T(4,128)S(1)}, s32[128,4]{0,1:T(4,128)}, u32[]{:S(2)}) copy-start(s32[128,4]{0,1:T(4,128)} %param.15) | copy-start | bytes 6148
  308.7 20.7 %copy-start.7 = (s32[64]{0:T(128)S(1)}, s32[64]{0:T(128)}, u32[]{:S(2)}) copy-start(s32[64]{0:T(128)} %param.16) | copy-start | bytes 772
  308.7 21.0 %copy-start.8 = (s32[64]{0:T(128)S(1)}, s32[64]{0:T(128)}, u32[]{:S(2)}) copy-start(s32[64]{0:T(128)} %param.17) | copy-start | bytes 772

commit v3 on v2

--- a/solution.py
+++ b/solution.py
@@ -27,99 +27,138 @@
 
 T_FIELDS = 7
 S_FIELDS = 8
-
-
-def pair_kernel(step_rows, tgt_ref, src_ref, adj_ref, dir_ref, image_ref, adjoint_ref, tile_ref):
+STEP_ROWS = 16
+STRIP = 512
+
+
+def pair_kernel(
+    step_rows,
+    strip,
+    tgt_ref,
+    src_ref,
+    adj_ref,
+    dir_ref,
+    dens_tgt_ref,
+    dens_src_ref,
+    tgt_wide,
+    src_wide,
+    dir_rows,
+    image_sum,
+    back_sum,
+    tile_ref,
+):
     j = pl.program_id(0)
     i = pl.program_id(1)
     rows_here, lanes_here = tile_ref.shape
-    for start in range(0, rows_here, step_rows):
-        rows = pl.ds(start, step_rows)
-
-        def column(field):
-            return tgt_ref[rows, field : field + 1]
-
-        def row(field):
-            full = src_ref[8 * field : 8 * field + 8, :]
-            return jnp.concatenate([full] * (step_rows // 8), axis=0)
-
-        tx, ty, tz, nx, ny, nz, tw = [column(f) for f in range(T_FIELDS)]
-        sx, sy, sz, sz4, sz2, sa, se, sk = [row(f) for f in range(S_FIELDS)]
-        delta_x = tx - sx
-        delta_y = ty - sy
-        delta_z = tz - sz
-        level = delta_x * delta_x + delta_y * delta_y + sa
-        near = level + delta_z * delta_z
-        mirror = near + tz * sz4
-        r_near = lax.rsqrt(near)
-        r_mirror = lax.rsqrt(mirror)
-        facing = nx * delta_x + ny * delta_y + nz * delta_z
-        facing_mirror = facing + nz * sz2
-        arc = level + MONIC[3]
-        arc = arc * level + MONIC[2]
-        arc = arc * level + MONIC[1]
-        arc = arc * level + MONIC[0]
-        arc = arc * level
-        arc = arc * (4.0 - arc)
-        arc = arc * (4.0 - arc)
-        arc = arc * (4.0 - arc)
-        total = (
-            facing * (r_near * r_near * r_near)
-            + facing_mirror * (r_mirror * r_mirror * r_mirror)
-            + (arc - 2.0) * (tw * se)
-        )
-        tile_ref[rows, :] = (total * sk).astype(jnp.bfloat16)
-
-    tile = tile_ref[...]
-    image = lax.dot_general(
-        tile, dir_ref[...], (((1,), (1,)), ((), ())), preferred_element_type=jnp.float32
-    )
-    back = jnp.dot(adj_ref[...], tile, preferred_element_type=jnp.float32)
-    out_rows = pl.ds(pl.multiple_of(i * rows_here, rows_here), rows_here)
+    wide = tgt_wide.shape[-1]
+
+    @pl.when(i == 0)
+    def _():
+        for field in range(S_FIELDS):
+            src_wide[8 * field : 8 * field + 8, :] = jnp.broadcast_to(
+                src_ref[0, field : field + 1, :], (8, lanes_here)
+            )
+        dir_rows[...] = dir_ref[0].astype(jnp.float32).T.astype(jnp.bfloat16)
+        back_sum[...] = jnp.zeros_like(back_sum)
 
     @pl.when(j == 0)
     def _():
-        image_ref[out_rows, :] = image
-
-    @pl.when(j > 0)
+        columns = tgt_ref[0].T
+        for field in range(T_FIELDS):
+            tgt_wide[i, field] = jnp.broadcast_to(
+                columns[:, field : field + 1], (rows_here, wide)
+            )
+        image_sum[i] = jnp.zeros(image_sum.shape[1:], jnp.float32)
+
+    def column(field, start):
+        part = tgt_wide[i, field, start : start + step_rows, :]
+        return jnp.concatenate([part] * (strip // wide), axis=1)
+
+    def row(field, at):
+        full = src_wide[8 * field : 8 * field + 8, at : at + strip]
+        return jnp.concatenate([full] * (step_rows // 8), axis=0)
+
+    for start in range(0, rows_here, step_rows):
+        for at in range(0, lanes_here, strip):
+            tx, ty, tz, nx, ny, nz, tw = [column(f, start) for f in range(T_FIELDS)]
+            sx, sy, sz, sz4, sz2, sa, se, sk = [row(f, at) for f in range(S_FIELDS)]
+            delta_x = tx - sx
+            delta_y = ty - sy
+            delta_z = tz - sz
+            level = delta_x * delta_x + delta_y * delta_y + sa
+            near = level + delta_z * delta_z
+            mirror = near + tz * sz4
+            r_near = lax.rsqrt(near)
+            r_mirror = lax.rsqrt(mirror)
+            facing = nx * delta_x + ny * delta_y + nz * delta_z
+            facing_mirror = facing + nz * sz2
+            arc = level + MONIC[3]
+            arc = arc * level + MONIC[2]
+            arc = arc * level + MONIC[1]
+            arc = arc * level + MONIC[0]
+            arc = arc * level
+            arc = arc * (4.0 - arc)
+            arc = arc * (4.0 - arc)
+            arc = arc * (4.0 - arc)
+            total = (
+                facing * (r_near * r_near * r_near)
+                + facing_mirror * (r_mirror * r_mirror * r_mirror)
+                + (arc - 2.0) * (tw * se)
+            )
+            tile_ref[start : start + step_rows, at : at + strip] = (total * sk).astype(
+                jnp.bfloat16
+            )
+
+    tile = tile_ref[...]
+    image_sum[i] += jnp.dot(tile, dir_rows[...], preferred_element_type=jnp.float32)
+    back_sum[...] += jnp.dot(adj_ref[0], tile, preferred_element_type=jnp.float32)
+
+    @pl.when(i == pl.num_programs(1) - 1)
     def _():
-        image_ref[out_rows, :] += image
-
-    @pl.when(i == 0)
+        dens_src_ref[0] = jnp.sum(
+            dir_ref[0].astype(jnp.float32) * back_sum[...], axis=0, keepdims=True
+        )
+
+    @pl.when(j == pl.num_programs(0) - 1)
     def _():
-        adjoint_ref[...] = back
-
-    @pl.when(i > 0)
-    def _():
-        adjoint_ref[...] += back
-
-
-def pair_images(tgt, src, adj_cols, dir_cols):
-    targets = tgt.shape[0]
-    sources = src.shape[1]
-    columns = dir_cols.shape[0]
-    rows_here = min(targets, 512)
-    lanes_here = min(sources, 512)
+        dens_tgt_ref[i] = jnp.sum(
+            adj_ref[0].astype(jnp.float32) * image_sum[i].T, axis=0, keepdims=True
+        )
+
+
+def pair_densities(tgt, src, adj, direct):
+    ncol, _, rows_here = tgt.shape
+    nrow, _, size = src.shape
+    columns = direct.shape[1]
+    lanes_here = min(size, 512)
+    cuts = size // lanes_here
     return pl.pallas_call(
-        functools.partial(pair_kernel, 16),
-        grid=(sources // lanes_here, targets // rows_here),
+        functools.partial(pair_kernel, min(rows_here, STEP_ROWS), min(lanes_here, STRIP)),
+        grid=(nrow * cuts, ncol),
         in_specs=[
-            pl.BlockSpec((rows_here, tgt.shape[1]), lambda j, i: (i, 0)),
-            pl.BlockSpec((src.shape[0], lanes_here), lambda j, i: (0, j)),
-            pl.BlockSpec((columns, rows_here), lambda j, i: (0, i)),
-            pl.BlockSpec((columns, lanes_here), lambda j, i: (0, j)),
+            pl.BlockSpec((1, tgt.shape[1], rows_here), lambda j, i: (i, 0, 0)),
+            pl.BlockSpec((1, src.shape[1], lanes_here), lambda j, i: (j // cuts, 0, j % cuts)),
+            pl.BlockSpec((1, columns, rows_here), lambda j, i: (i, 0, 0)),
+            pl.BlockSpec((1, columns, lanes_here), lambda j, i: (j // cuts, 0, j % cuts)),
         ],
         out_specs=[
-            pl.BlockSpec((targets, columns), lambda j, i: (0, 0)),
-            pl.BlockSpec((columns, lanes_here), lambda j, i: (0, j)),
+            pl.BlockSpec((ncol, 1, rows_here), lambda j, i: (0, 0, 0)),
+            pl.BlockSpec((1, 1, lanes_here), lambda j, i: (j // cuts, 0, j % cuts)),
         ],
         out_shape=[
-            jax.ShapeDtypeStruct((targets, columns), jnp.float32),
-            jax.ShapeDtypeStruct((columns, sources), jnp.float32),
-        ],
-        scratch_shapes=[pltpu.VMEM((rows_here, lanes_here), jnp.bfloat16)],
+            jax.ShapeDtypeStruct((ncol, 1, rows_here), jnp.float32),
+            jax.ShapeDtypeStruct((nrow, 1, size), jnp.float32),
+        ],
+        scratch_shapes=[
+            pltpu.VMEM((ncol, T_FIELDS, rows_here, min(lanes_here, 128)), jnp.float32),
+            pltpu.VMEM((8 * S_FIELDS, lanes_here), jnp.float32),
+            pltpu.VMEM((lanes_here, columns), jnp.bfloat16),
+            pltpu.VMEM((ncol, rows_here, columns), jnp.float32),
+            pltpu.VMEM((columns, lanes_here), jnp.float32),
+            pltpu.VMEM((rows_here, lanes_here), jnp.bfloat16),
+        ],
         name="pair_images",
-    )(tgt, src, adj_cols, dir_cols)
+    )(tgt, src, adj, direct)
 
 
 MESH = pl.DeviceIdType.MESH
@@ -363,20 +402,8 @@
     tgt_all, adj_all, src_all, dir_all = gather_all(
         nrow, ncol, tgt_fields, adjoint.T, src_fields, direct.T
     )
-
-    def beside(chunks):
-        return jnp.swapaxes(chunks, 0, 1).reshape(chunks.shape[1], -1)
-
-    tgt = jnp.swapaxes(tgt_all, 1, 2).reshape(-1, tgt_all.shape[1])
-    src = jnp.repeat(beside(src_all), 8, axis=0)
-    adj_cols = beside(adj_all)
-    dir_cols = beside(dir_all)
-    image, back = pair_images(tgt, src, adj_cols, dir_cols)
-    dens_tgt = jnp.sum(adj_cols.astype(jnp.float32) * image.T, axis=0)
-    dens_src = jnp.sum(dir_cols.astype(jnp.float32) * back, axis=0)
-    densities, every_density = sum_densities(
-        nrow, ncol, dens_tgt.reshape(ncol, 1, size), dens_src.reshape(nrow, 1, size)
-    )
+    dens_tgt, dens_src = pair_densities(tgt_all, src_all, adj_all, dir_all)
+    densities, every_density = sum_densities(nrow, ncol, dens_tgt, dens_src)
     densities = densities.reshape(size)
     blocks = every_density.reshape(NBLK, BPAN)
     ends = jnp.cumsum(patch_counts)

time: 345 us -> 299 us (0.87)
  Pallas kernels: 321 us -> 288 us
  local copies, waits for them, and re-layouts: 13.7 us -> 6.11 us
  other arithmetic: 6.91 us -> 2.3 us
    pallas_call x1, Pallas kernels: 275 us -> 242 us  [pair_densities(): pl.pallas_call(functools.partial(pair_kernel, min(rows_here, STEP_ROWS),...]
    reshape x3 -> x0, local copies, waits for them, and re-layouts: 4.76 us -> none  [the longest x2 3.28 us: beside(): return jnp.swapaxes(chunks, 0, 1).reshape(chunks.shape[1], -1)]
where the time goes in v3:
time: 299 us
  Pallas kernels  288 us (96%)
  local copies, waits for them, and re-layouts  6.11 us (2%)
    pallas_call x1, Pallas kernels, pair_densities(): pl.pallas_call(functools.partial(pair_kernel, min(rows_here, STEP_ROWS),...  242 us
    pallas_call x1, Pallas kernels, gather_all(): pl.pallas_call(functools.partial(gather_kernel, nrow, ncol), in_specs=[an...  19.9 us
    pallas_call x1, Pallas kernels, sum_densities(): pl.pallas_call(functools.partial(density_kernel, nrow, ncol), in_specs=[v...  16.4 us
    pallas_call x1, Pallas kernels, sum_patches(): pl.pallas_call(functools.partial(patch_kernel, nrow, ncol), in_specs=[vme...  10.2 us

profile of v3, /device:TPU:0, one launch (start us, length us, event | category | flops | bytes accessed | tf_op | source)
XLA Modules:
  0.0 298.7 jit_solution(15735499549570777921)
XLA Ops:
  0.6 0.0 copy-start
  0.6 0.0 copy-start.3
  0.7 0.8 multiply_exponential_fusion
  1.5 0.0 copy-start.2
  1.5 0.0 copy-done.3
  1.5 0.7 copy-done.2
  2.2 0.0 copy-start.1
  2.2 0.7 concatenate.7.src_ref
  2.9 0.1 copy-done.1
  2.9 0.6 concatenate.6.tgt_ref
  3.5 19.9 %gather_all.1 = (f32[4,8,1024]{2,1,0:T(8,128)}, bf16[4,64,1024]{2,1,0:T(8,128)(2,1)}, f32[8,8,1024]{2,1,0:T(8,128)}, bf16[8,64,1024]{2,1,0:T(8,128)(2,1)}) custom-call(f32[8,1024]{1,0:T(8,128)} %concatenate.6.tgt_ref, bf16[64,1024]{1,0:T(8,128)(2,1)} %bitcast.15, f32[8,1024]{1,0:T(8,128)} %concatenate.7.src_ref, bf16[64,1024]{1,0:T(8,128)(2,1)} %bitcast.16), custom_call_target="tpu_custom_call" | custom-call | tf_op jit(solution)/shard_map/gather_all/pallas_call | solution.py:236
  23.4 241.8 %pair_images.1 = (f32[4,1,1024]{2,1,0:T(1,128)}, f32[8,1,1024]{2,1,0:T(1,128)}) custom-call(f32[4,8,1024]{2,1,0:T(8,128)} %get-tuple-element.10.tgt_ref, f32[8,8,1024]{2,1,0:T(8,128)} %get-tuple-element.11.src_ref, bf16[4,64,1024]{2,1,0:T(8,128)(2,1)} %get-tuple-element.12.adj_ref, bf16[8,64,1024]{2,1,0:T(8,128)(2,1)} %get-tuple-element.13.dir_ref), custom_call_target="tpu_custom_call" | custom-call | tf_op jit(solution)/shard_map/pair_images/pallas_call | solution.py:135
  265.2 16.4 %sum_densities.1 = (f32[1,1024]{1,0:T(1,128)}, f32[8,4,1,1024]{3,2,1,0:T(1,128)}) custom-call(f32[4,1,1024]{2,1,0:T(1,128)} %get-tuple-element.14.tgt_ref, f32[8,1,1024]{2,1,0:T(1,128)} %get-tuple-element.15.src_ref), custom_call_target="tpu_custom_call" | custom-call | tf_op jit(solution)/shard_map/sum_densities/pallas_call | solution.py:297
  281.6 1.2 reduce.1
  282.8 0.1 reshape.46
  282.9 0.0 copy-start.5
  282.9 0.7 copy-done.5
  283.6 0.0 copy-start.6
  283.6 0.6 copy-done.6
  284.3 0.1 copy.12
  284.4 0.1 reduce-window.8
  284.5 0.1 reduce
  284.6 0.0 copy-start.7
  284.6 0.6 copy-done.7
  285.2 0.2 fusion
  285.4 0.2 fusion.8
  285.7 0.0 copy-done
  285.7 0.9 fusion.1.part_ref
  286.6 0.0 copy-start.4
  286.6 10.2 %sum_patches.1 = f32[8,512]{1,0:T(8,128)} custom-call(f32[8,8,512]{2,1,0:T(8,128)} %fusion.1.part_ref), custom_call_target="tpu_custom_call" | custom-call | tf_op jit(solution)/shard_map/sum_patches/pallas_call | solution.py:345
  296.8 0.0 copy-done.4
  296.8 0.6 copy.15
  297.4 1.3 copy.16
  (6 shorter events, 0.0 us)
Async XLA Ops:
  0.6 285.0 %copy-start = (bf16[1,256,512]{2,1,0:T(8,128)(2,1)S(1)}, bf16[1,256,512]{2,1,0:T(8,128)(2,1)}, u32[]{:S(2)}) copy-start(bf16[1,256,512]{2,1,0:T(8,128)(2,1)} %param.14) | copy-start | bytes 786436
  0.6 0.8 copy-start.3
  1.5 0.7 copy-start.2
  2.2 0.7 copy-start.1
  282.9 0.7 copy-start.5
  283.6 0.7 copy-start.6
  284.6 0.7 copy-start.7
  286.6 10.2 %copy-start.4 = (f32[1,1024]{1,0:T(1,128)S(1)}, f32[1,1024]{1,0:T(1,128)}, u32[]{:S(2)}) copy-start(f32[1,1024]{1,0:T(1,128)} %get-tuple-element.16) | copy-start | bytes 12292

commit v4 on v3

--- a/solution.py
+++ b/solution.py
@@ -15,15 +15,9 @@
 wave_number = 6.0
 inv_four_pi = 0.07957747154594767
 
-HALF_ANGLE = (
-    0.5624999387637301,
-    -0.026367050589663217,
-    0.0004942961270241117,
-    -4.941951390951122e-06,
-    2.8141817781696455e-08,
-)
-SQ_SCALE = HALF_ANGLE[-1] ** (1.0 / len(HALF_ANGLE))
-MONIC = tuple(c / SQ_SCALE ** (i + 1) for i, c in enumerate(HALF_ANGLE[:-1]))
+PART_ANGLE = (0.049382699279181326, -0.00020320446239655373, 3.3039392806237825e-07)
+SQ_SCALE = PART_ANGLE[-1] ** (1.0 / len(PART_ANGLE))
+MONIC = tuple(c / SQ_SCALE ** (i + 1) for i, c in enumerate(PART_ANGLE[:-1]))
 
 T_FIELDS = 7
 S_FIELDS = 8
@@ -92,14 +86,12 @@
             r_mirror = lax.rsqrt(mirror)
             facing = nx * delta_x + ny * delta_y + nz * delta_z
             facing_mirror = facing + nz * sz2
-            arc = level + MONIC[3]
-            arc = arc * level + MONIC[2]
-            arc = arc * level + MONIC[1]
+            arc = level + MONIC[1]
             arc = arc * level + MONIC[0]
             arc = arc * level
-            arc = arc * (4.0 - arc)
-            arc = arc * (4.0 - arc)
-            arc = arc * (4.0 - arc)
+            for _ in range(3):
+                rest = 3.0 - arc
+                arc = arc * (rest * rest)
             total = (
                 facing * (r_near * r_near * r_near)
                 + facing_mirror * (r_mirror * r_mirror * r_mirror)

time: 299 us -> 296 us (0.990)
  Pallas kernels: 288 us -> 285 us
    pallas_call x1, Pallas kernels: 242 us -> 239 us  [pair_densities(): pl.pallas_call(functools.partial(pair_kernel, min(rows_here, STEP_ROWS),...]
where the time goes in v4:
time: 296 us
  Pallas kernels  285 us (96%)
  local copies, waits for them, and re-layouts  6.11 us (2%)
    pallas_call x1, Pallas kernels, pair_densities(): pl.pallas_call(functools.partial(pair_kernel, min(rows_here, STEP_ROWS),...  239 us
    pallas_call x1, Pallas kernels, gather_all(): pl.pallas_call(functools.partial(gather_kernel, nrow, ncol), in_specs=[an...  19.9 us
    pallas_call x1, Pallas kernels, sum_densities(): pl.pallas_call(functools.partial(density_kernel, nrow, ncol), in_specs=[v...  16.4 us
    pallas_call x1, Pallas kernels, sum_patches(): pl.pallas_call(functools.partial(patch_kernel, nrow, ncol), in_specs=[vme...  10.2 us

profile of v4, /device:TPU:0, one launch (start us, length us, event | category | flops | bytes accessed | tf_op | source)
XLA Modules:
  0.0 295.7 jit_solution(9366963827849013210)
XLA Ops:
  0.6 0.0 copy-start
  0.6 0.0 copy-start.3
  0.7 0.8 multiply_exponential_fusion
  1.5 0.0 copy-start.2
  1.5 0.0 copy-done.3
  1.5 0.7 copy-done.2
  2.2 0.0 copy-start.1
  2.2 0.7 concatenate.7.src_ref
  2.9 0.1 copy-done.1
  2.9 0.6 concatenate.6.tgt_ref
  3.5 19.9 %gather_all.1 = (f32[4,8,1024]{2,1,0:T(8,128)}, bf16[4,64,1024]{2,1,0:T(8,128)(2,1)}, f32[8,8,1024]{2,1,0:T(8,128)}, bf16[8,64,1024]{2,1,0:T(8,128)(2,1)}) custom-call(f32[8,1024]{1,0:T(8,128)} %concatenate.6.tgt_ref, bf16[64,1024]{1,0:T(8,128)(2,1)} %bitcast.15, f32[8,1024]{1,0:T(8,128)} %concatenate.7.src_ref, bf16[64,1024]{1,0:T(8,128)(2,1)} %bitcast.16), custom_call_target="tpu_custom_call" | custom-call | tf_op jit(solution)/shard_map/gather_all/pallas_call | solution.py:228
  23.4 238.7 %pair_images.1 = (f32[4,1,1024]{2,1,0:T(1,128)}, f32[8,1,1024]{2,1,0:T(1,128)}) custom-call(f32[4,8,1024]{2,1,0:T(8,128)} %get-tuple-element.10.tgt_ref, f32[8,8,1024]{2,1,0:T(8,128)} %get-tuple-element.11.src_ref, bf16[4,64,1024]{2,1,0:T(8,128)(2,1)} %get-tuple-element.12.adj_ref, bf16[8,64,1024]{2,1,0:T(8,128)(2,1)} %get-tuple-element.13.dir_ref), custom_call_target="tpu_custom_call" | custom-call | tf_op jit(solution)/shard_map/pair_images/pallas_call | solution.py:127
  262.1 16.4 %sum_densities.1 = (f32[1,1024]{1,0:T(1,128)}, f32[8,4,1,1024]{3,2,1,0:T(1,128)}) custom-call(f32[4,1,1024]{2,1,0:T(1,128)} %get-tuple-element.14.tgt_ref, f32[8,1,1024]{2,1,0:T(1,128)} %get-tuple-element.15.src_ref), custom_call_target="tpu_custom_call" | custom-call | tf_op jit(solution)/shard_map/sum_densities/pallas_call | solution.py:289
  278.5 1.2 reduce.1
  279.8 0.1 reshape.46
  279.9 0.0 copy-start.5
  279.9 0.7 copy-done.5
  280.6 0.0 copy-start.6
  280.6 0.6 copy-done.6
  281.2 0.1 copy.12
  281.3 0.1 reduce-window.8
  281.4 0.1 reduce
  281.5 0.0 copy-start.7
  281.6 0.6 copy-done.7
  282.2 0.2 fusion
  282.4 0.2 fusion.8
  282.6 0.0 copy-done
  282.6 0.9 fusion.1.part_ref
  283.5 0.0 copy-start.4
  283.5 10.2 %sum_patches.1 = f32[8,512]{1,0:T(8,128)} custom-call(f32[8,8,512]{2,1,0:T(8,128)} %fusion.1.part_ref), custom_call_target="tpu_custom_call" | custom-call | tf_op jit(solution)/shard_map/sum_patches/pallas_call | solution.py:337
  293.8 0.0 copy-done.4
  293.8 0.6 copy.15
  294.4 1.3 copy.16
  (6 shorter events, 0.0 us)
Async XLA Ops:
  0.6 282.0 %copy-start = (bf16[1,256,512]{2,1,0:T(8,128)(2,1)S(1)}, bf16[1,256,512]{2,1,0:T(8,128)(2,1)}, u32[]{:S(2)}) copy-start(bf16[1,256,512]{2,1,0:T(8,128)(2,1)} %param.14) | copy-start | bytes 786436
  0.6 0.8 copy-start.3
  1.5 0.7 copy-start.2
  2.2 0.7 copy-start.1
  279.9 0.7 copy-start.5
  280.6 0.7 copy-start.6
  281.5 0.7 copy-start.7
  283.5 10.2 %copy-start.4 = (f32[1,1024]{1,0:T(1,128)S(1)}, f32[1,1024]{1,0:T(1,128)}, u32[]{:S(2)}) copy-start(f32[1,1024]{1,0:T(1,128)} %get-tuple-element.16) | copy-start | bytes 12292
